TPU v7x, 32 devices: a whole 2x2x4 slice. The times are simulated.
32 devices in a mesh: seg: 4 (over y, x), slab: 8 (over z, core).
Axes of the slice: x: 2, y: 2, z: 4, core: 2. Of those that a mesh axis runs over, the one named last changes fastest.
Arguments:
- positions: bfloat16 [4, 32, 3, 642], P('seg', 'slab'), may hold values from -6 to 6
- density: bfloat16 [4, 32, 3, 642], P('seg', 'slab'), may hold values from -6 to 6
- upsample: bfloat16 [642, 2562], replicated, may hold values from -0.25 to 0.25
- quad_weights: float32 [2562], replicated, may hold values from 0.3 to 3
- coarse_weights: float32 [642], replicated, may hold values from 0.3 to 3
- pair_target: int32 [4, 16], P('seg', 'slab'), may hold values from 0 to 3
- pair_source: int32 [4, 16], P('seg', 'slab'), may hold values from 0 to 7
- junction_cell: int32 [4, 8, 4], P('seg', 'slab'), may hold values from 0 to 3
- junction_target: int32 [4, 8, 4], P('seg', 'slab'), may hold values from 0 to 3
- wall_points: bfloat16 [4, 8, 3, 128], P('seg', 'slab'), may hold values from -6 to 6
- wall_traction: bfloat16 [4, 8, 3, 128], P('seg', 'slab'), may hold values from -6 to 6
- wall_near: int32 [4, 32, 2], P('seg', 'slab'), may hold values from 0 to 7
Outputs:
- velocity: float32 [4, 32, 3, 642], P('seg', 'slab')
All inputs are finite; a program needn't handle non-finite values.
Results may differ from a plain program's by a relative error of at most 0.0024.
Values may be sent and summed in bfloat16 or wider, within the bound.
A program may use at most 64 MiB of HBM per device.

v0:
```python
import functools
import math

import jax
import jax.numpy as jnp
from jax import lax
from jax.experimental import pallas as pl
from jax.experimental.pallas import tpu as pltpu
from jax.sharding import PartitionSpec as P

MESH = pl.DeviceIdType.MESH
HALO = 2
EPSILON2 = 0.05
WALL_GAIN = 3.0
LANES = 128
TERMS = 16
MOST = 7
KAPPA = 1.0 / EPSILON2
F32 = jnp.float32
BF16 = jnp.bfloat16


def up(n, m):
    return -(-n // m) * m


def split(value, parts):
    out = []
    for _ in range(parts):
        piece = value.astype(BF16).astype(F32)
        out.append(piece)
        value = value - piece
    return out


def kernel(
    cfg,
    pair_target_far, pair_source_far, junction_cell_far, junction_target_far, wall_near_far,
    positions, density, upsample, quad_far, coarse_far, wall_points, wall_traction,
    out,
    pair_target, pair_source, junction_cell, junction_target, wall_near, quad, coarse,
    own, low, high, jsend, jrecv, walls, ups, rows, lhs, fine, ysrc, gsrc, yd, yg, ga, gb, xt, xs, wide, acc,
    local_sem, halo_send, halo_recv, junction_send, junction_recv, wall_send, wall_recv,
):
    count, points, fine_points, pairs, near, patch, segs, slabs, per_slab = cfg
    pt, qp = up(points, LANES), up(fine_points, LANES)
    rows_t = up(points, 16)
    seg, slab = lax.axis_index("seg"), lax.axis_index("slab")

    barrier = pltpu.get_barrier_semaphore()
    for o in range(1, segs):
        pl.semaphore_signal(barrier, inc=1, device_id={"seg": lax.rem(seg + o, segs)}, device_id_type=MESH)
    for o in range(1, slabs):
        pl.semaphore_signal(barrier, inc=1, device_id={"slab": lax.rem(slab + o, slabs)}, device_id_type=MESH)

    copies = [
        pltpu.make_async_copy(positions.at[0], own.at[0], local_sem.at[0]),
        pltpu.make_async_copy(density.at[0], own.at[1], local_sem.at[1]),
        pltpu.make_async_copy(wall_points.at[0], walls.at[pl.ds(slab * per_slab, per_slab), 0], local_sem.at[2]),
        pltpu.make_async_copy(wall_traction.at[0], walls.at[pl.ds(slab * per_slab, per_slab), 1], local_sem.at[3]),
    ]
    big = pltpu.make_async_copy(upsample, ups, local_sem.at[4])
    tables = [
        pltpu.make_async_copy(source, target, local_sem.at[5 + i]) for i, (source, target) in enumerate([
            (pair_target_far, pair_target), (pair_source_far, pair_source), (junction_cell_far, junction_cell),
            (junction_target_far, junction_target), (wall_near_far, wall_near), (quad_far, quad), (coarse_far, coarse)])
    ]
    for copy in copies + tables:
        copy.start()
    big.start()

    for copy in copies + tables:
        copy.wait()
    cell_at = lax.broadcasted_iota(jnp.int32, (count, points), 0)

    def pick(kind, i, near_by):
        total = jnp.zeros((count, points), F32)
        for ref, first in near_by:
            total = total + jnp.where(cell_at == first, ref[kind, i].astype(F32), 0.0)
        return jnp.sum(total, axis=0, keepdims=True)

    for b in range(segs):
        mine = junction_cell[0, 0, b]
        jsend[b] = jnp.concatenate(
            [pick(kind, i, [(own, mine)]) for kind in range(2) for i in range(3)], axis=0).astype(BF16)
    ysrc[...] = jnp.zeros_like(ysrc)
    gsrc[...] = jnp.zeros_like(gsrc)

    @pl.when(slab == 0)
    def _():
        low[...] = jnp.zeros_like(low)

    @pl.when(slab == slabs - 1)
    def _():
        high[...] = jnp.zeros_like(high)

    rows[...] = jnp.zeros_like(rows)
    coords = [own[0, i].astype(F32) for i in range(3)]
    norms = split(KAPPA * (coords[0] * coords[0] + coords[1] * coords[1] + coords[2] * coords[2]), 3)
    rows[9:12, 0:points] = jnp.ones((3, points), F32)
    def target_rows(c):
        for i in range(3):
            line = coords[i][c:c + 1]
            xs[c, i:i + 1] = line
            rows[i:i + 1, 0:points] = line
            rows[3 + i:4 + i, 0:points] = line
            rows[6 + i:7 + i, 0:points] = norms[i][c:c + 1]
        turned = rows[...].T[0:rows_t]
        xt[c] = turned.astype(BF16)
        for i in range(3):
            wide[c, i] = jnp.broadcast_to(turned[:, i:i + 1], (rows_t, LANES))
        acc[c] = jnp.zeros(acc.shape[1:], F32)

    for c in range(count // 2):
        target_rows(c)
    pl.semaphore_wait(barrier, segs - 1 + slabs - 1)

    def halo_up():
        return pltpu.make_async_remote_copy(
            own, low, halo_send.at[0], halo_recv.at[0],
            device_id={"slab": lax.rem(slab + 1, slabs)}, device_id_type=MESH)

    def halo_down():
        return pltpu.make_async_remote_copy(
            own, high, halo_send.at[1], halo_recv.at[1],
            device_id={"slab": lax.rem(slab + slabs - 1, slabs)}, device_id_type=MESH)

    def junction(o):
        return pltpu.make_async_remote_copy(
            jsend.at[lax.rem(seg + o, segs)], jrecv.at[seg], junction_send.at[o], junction_recv.at[o],
            device_id={"seg": lax.rem(seg + o, segs)}, device_id_type=MESH)

    def junction_in(o):
        return pltpu.make_async_remote_copy(
            jsend.at[seg], jrecv.at[lax.rem(seg + segs - o, segs)], junction_send.at[o], junction_recv.at[o],
            device_id={"seg": lax.rem(seg + o, segs)}, device_id_type=MESH)

    def wall(o, of):
        slot = pl.ds(of * per_slab, per_slab)
        return pltpu.make_async_remote_copy(
            walls.at[slot], walls.at[slot], wall_send.at[o], wall_recv.at[o],
            device_id={"slab": lax.rem(slab + o, slabs)}, device_id_type=MESH)

    @pl.when(slab < slabs - 1)
    def _():
        halo_up().start()

    @pl.when(slab > 0)
    def _():
        halo_down().start()

    for o in range(1, segs):
        junction(o).start()
    for o in range(slabs - 1, 0, -1):
        wall(o, slab).start()

    for c in range(count // 2, count):
        target_rows(c)

    def prepare(start, size):
        at = pl.ds(start, size)
        y, g = ysrc[0:3, at], gsrc[0:3, at]
        g_hi, g_lo = split(g, 2)
        y_hi, y_lo = split((-2.0 * KAPPA) * y, 2)
        norm = split(KAPPA * jnp.sum(y * y, axis=0, keepdims=True) + 1.0, 3)
        dot = -jnp.sum(y * (g_hi + g_lo), axis=0, keepdims=True)
        gsrc[0:3, at] = g_hi + g_lo
        gsrc[3:4, at] = dot
        dot = split(dot, 3)
        one = jnp.ones((3, size), F32)
        none = jnp.zeros((3, size), F32)
        pad = jnp.zeros((TERMS - 12, size), F32)
        yd[:, at] = jnp.concatenate([y_hi, y_lo, one] + norm + [pad], axis=0).astype(BF16)
        yg[:, at] = jnp.concatenate([g_hi, g_lo, none] + dot + [pad], axis=0).astype(BF16)
        ga[:, at] = jnp.concatenate([one[0:1], y, jnp.zeros((TERMS - 4, size), F32)], axis=0).astype(BF16)
        gb[:, at] = jnp.concatenate([jnp.zeros((TERMS - 8, size), F32), g_hi, g_lo, none[0:2]], axis=0).astype(BF16)

    def finish(distance, along, at):
        inverse = lax.rsqrt(distance)
        inverse3 = inverse * inverse * inverse
        return lax.dot_general(
            jnp.concatenate([ga[:, at], gb[:, at]], axis=1),
            jnp.concatenate([(along * inverse3).astype(BF16), (inverse + inverse3).astype(BF16)], axis=1),
            (((1,), (1,)), ((), ())), preferred_element_type=F32)

    def group(target, start, size):
        targets = xt[target]
        ats = [pl.ds(pl.multiple_of(start + i * LANES, LANES), LANES) for i in range(size)]
        total = None
        single = {7: 3, 6: 2}.get(size, size % 2)
        for i in range(0, size - single, 2):
            pair = jnp.dot(
                targets, jnp.concatenate([yd[:, ats[i]], yd[:, ats[i + 1]]], axis=1), preferred_element_type=F32)
            for at, distance in ((ats[i], pair[:, :LANES]), (ats[i + 1], pair[:, LANES:])):
                along = gsrc[3:4, at] + wide[target, 0] * gsrc[0:1, at]
                along = along + wide[target, 1] * gsrc[1:2, at]
                along = along + wide[target, 2] * gsrc[2:3, at]
                term = finish(distance, along, at)
                total = term if total is None else total + term
        for at in ats[size - single:]:
            both = jnp.dot(
                targets, jnp.concatenate([yd[:, at], yg[:, at]], axis=1), preferred_element_type=F32)
            term = finish(both[:, :LANES], both[:, LANES:], at)
            total = term if total is None else total + term
        return total

    def block(target, start, chunks):
        size = max(n for n in range(1, 8) if chunks % n == 0)

        def step(i, total):
            return total + group(target, start + i * size * LANES, size)

        if chunks == size:
            return group(target, start, size)
        return lax.fori_loop(0, chunks // size, step, jnp.zeros((TERMS, rows_t), F32))

    def add(target, value):
        for c in range(count):
            acc[c] = acc[c] + jnp.where(target == c, 1.0, 0.0) * value

    @pl.when(slab > 0)
    def _():
        halo_up().wait_recv()

    @pl.when(slab < slabs - 1)
    def _():
        halo_down().wait_recv()

    for k in range(pairs):
        source = pair_source[0, k]
        around = [(low, source + (count - HALO)), (own, source - HALO), (high, source - (HALO + count))]
        for kind in range(2):
            for i in range(3):
                lhs[6 * k + 3 * kind + i:6 * k + 3 * kind + i + 1] = pick(kind, i, around)
    big.wait()
    fine[...] = jnp.dot(lhs[...].astype(BF16), ups[...], preferred_element_type=F32).astype(BF16).astype(F32)
    for k in range(pairs):
        ysrc[0:3, pl.ds(k * qp, fine_points)] = fine[6 * k:6 * k + 3]
        gsrc[0:3, pl.ds(k * qp, fine_points)] = fine[6 * k + 3:6 * k + 6] * quad[...][None]
    prepare(0, pairs * qp)
    size = max(n for n in range(1, MOST + 1) if (qp // LANES) % n == 0)

    def together(i, totals):
        return tuple(
            total + group(pair_target[0, k], k * qp + i * size * LANES, size) for k, total in enumerate(totals))

    zero = jnp.zeros((TERMS, rows_t), F32)
    totals = lax.fori_loop(0, qp // LANES // size, together, (zero,) * pairs)
    for k in range(pairs):
        add(pair_target[0, k], totals[k])

    base = pairs * qp
    for o in range(1, segs):
        junction_in(o).wait_recv()
        source = jrecv[lax.rem(seg + segs - o, segs)]
        at = pl.ds(base + (o - 1) * pt, points)
        ysrc[0:3, at] = source[0:3].astype(F32)
        gsrc[0:3, at] = source[3:6].astype(F32) * coarse[...][None]
    prepare(base, (segs - 1) * pt)
    for o in range(1, segs):
        target = junction_target[0, 0, lax.rem(seg + segs - o, segs)]
        add(target, block(target, base + (o - 1) * pt, pt // LANES))

    base = base + (segs - 1) * pt
    for o in range(1, slabs):
        wall(o, lax.rem(slab + slabs - o, slabs)).wait_recv()
    width = up(patch, LANES)
    for c in range(count):
        for n in range(near):
            source = walls[wall_near[0, n, c]]
            at = pl.ds(base + (c * near + n) * width, patch)
            ysrc[0:3, at] = source[0].astype(F32)
            gsrc[0:3, at] = source[1].astype(F32) * WALL_GAIN
    prepare(base, count * near * width)
    scale = 1.0 / (math.sqrt(EPSILON2) * 8.0 * math.pi)
    for c in range(count):
        total = (acc[c] + block(c, base + c * near * width, near * width // LANES))[:, 0:points]
        x = xs[c, 0:3]
        value = scale * (total[8:11] + total[11:14] + KAPPA * (x * total[0:1] - total[1:4]))
        for i in range(3):
            out[0, i, c:c + 1] = value[i:i + 1]

    @pl.when(slab < slabs - 1)
    def _():
        halo_up().wait_send()

    @pl.when(slab > 0)
    def _():
        halo_down().wait_send()

    for o in range(1, segs):
        junction(o).wait_send()
    for o in range(1, slabs):
        wall(o, slab).wait_send()


def local(segs, slabs, positions, density, upsample, quad_weights, coarse_weights, pair_target, pair_source,
          junction_cell, junction_target, wall_points, wall_traction, wall_near):
    count, points = positions.shape[1], positions.shape[3]
    turned = (1, 3, count, points)
    fine_points = upsample.shape[1]
    pairs, near = pair_target.shape[1], wall_near.shape[2]
    per_slab, patch = wall_points.shape[1], wall_points.shape[3]
    cfg = (count, points, fine_points, pairs, near, patch, segs, slabs, per_slab)
    pt, qp = up(points, LANES), up(fine_points, LANES)
    lanes = pairs * qp + (segs - 1) * pt + count * near * up(patch, LANES)
    vmem = pl.BlockSpec(memory_space=pltpu.VMEM)
    far = pl.BlockSpec(memory_space=pl.ANY)
    dma = pltpu.SemaphoreType.DMA
    result = pl.pallas_call(
        functools.partial(kernel, cfg),
        out_shape=jax.ShapeDtypeStruct(turned, F32),
        in_specs=[far] * 12,
        out_specs=vmem,
        scratch_shapes=[
            pltpu.SMEM(pair_target.shape, jnp.int32),
            pltpu.SMEM(pair_source.shape, jnp.int32),
            pltpu.SMEM(junction_cell.shape, jnp.int32),
            pltpu.SMEM(junction_target.shape, jnp.int32),
            pltpu.SMEM((1, near, count), jnp.int32),
            pltpu.VMEM(quad_weights.shape, F32),
            pltpu.VMEM(coarse_weights.shape, F32),
            pltpu.VMEM((2,) + turned[1:], BF16),
            pltpu.VMEM((2,) + turned[1:], BF16),
            pltpu.VMEM((2,) + turned[1:], BF16),
            pltpu.VMEM((segs, 6, points), BF16),
            pltpu.VMEM((segs, 6, points), BF16),
            pltpu.VMEM((slabs * per_slab, 2, 3, patch), BF16),
            pltpu.VMEM(upsample.shape, BF16),
            pltpu.VMEM((TERMS, pt), F32),
            pltpu.VMEM((6 * pairs, points), F32),
            pltpu.VMEM((6 * pairs, fine_points), F32),
            pltpu.VMEM((8, lanes), F32),
            pltpu.VMEM((8, lanes), F32),
            pltpu.VMEM((TERMS, lanes), BF16),
            pltpu.VMEM((TERMS, lanes), BF16),
            pltpu.VMEM((TERMS, lanes), BF16),
            pltpu.VMEM((TERMS, lanes), BF16),
            pltpu.VMEM((count, up(points, 16), TERMS), BF16),
            pltpu.VMEM((count, 3, points), F32),
            pltpu.VMEM((count, 3, up(points, 16), LANES), F32),
            pltpu.VMEM((count, TERMS, up(points, 16)), F32),
            dma((12,)), dma((2,)), dma((2,)), dma((segs,)), dma((segs,)), dma((slabs,)), dma((slabs,)),
        ],
        compiler_params=pltpu.CompilerParams(collective_id=0, has_side_effects=True),
    )(pair_target, pair_source, junction_cell, junction_target, wall_near.transpose(0, 2, 1),
      positions.transpose(0, 2, 1, 3), density.transpose(0, 2, 1, 3), upsample, quad_weights, coarse_weights,
      wall_points, wall_traction)
    return result.transpose(0, 2, 1, 3)


def solution(mesh):
    placed = (
        P("seg", "slab", None, None),
        P("seg", "slab", None, None),
        P(),
        P(),
        P(),
        P("seg", "slab"),
        P("seg", "slab"),
        P("seg", "slab", None),
        P("seg", "slab", None),
        P("seg", "slab", None, None),
        P("seg", "slab", None, None),
        P("seg", "slab", None),
    )
    body = functools.partial(local, mesh.shape["seg"], mesh.shape["slab"])
    return jax.shard_map(
        body, mesh=mesh, in_specs=placed, out_specs=P("seg", "slab", None, None), check_vma=False
    )
```

profile of v0, /device:TPU:1, one launch (start us, length us, event | category | flops | bytes accessed | tf_op | source)
XLA Modules:
  0.0 23.4 jit_solution(6047436281118966045)
XLA Ops:
  0.0 22.0 %shard_map.118 = f32[1,3,4,642]{3,2,1,0:T(4,128)} custom-call(s32[1,2]{1,0:T(1,128)} %pair_target_far.1, s32[1,2]{1,0:T(1,128)} %pair_source_far.1, s32[1,1,4]{2,1,0:T(1,128)} %junction_cell_far.1, s32[1,1,4]{2,1,0:T(1,128)} %junction_target_far.1, s32[1,2,4]{2,1,0:T(2,128)} %bitcast.7, bf16[1,3,4,642]{3,2,1,0:T(4,128)(2,1)} %bitcast.5, ...), custom_call_target="tpu_custom_call" | custom-call | tf_op jit(solution)/shard_map/pallas_call | solution.py:310
  22.0 1.4 %copy.14 = f32[1,4,3,642]{3,1,2,0:T(4,128)} copy(f32[1,4,3,642]{3,1,2,0:T(4,128)} %bitcast.4) | data formatting | bytes 61632
where the time goes:
time: 23.5 us; the launch traced here: 23.4 us
  Pallas kernels  22 us (94%)
  local copies, waits for them, and re-layouts  1.39 us (6%)
    pallas_call x1, Pallas kernels, local(): pl.pallas_call(functools.partial(kernel, cfg), out_shape=jax.ShapeDtypeSt...  22 us
    unnamed x1, local copies, waits for them, and re-layouts  1.39 us

commit v1 on v0

v1 whole, which is shorter than its diff:
```python
import functools
import math

import jax
import jax.numpy as jnp
from jax import lax
from jax.experimental import pallas as pl
from jax.experimental.pallas import tpu as pltpu
from jax.sharding import PartitionSpec as P

MESH = pl.DeviceIdType.MESH
HALO = 2
EPSILON2 = 0.05
WALL_GAIN = 3.0
LANES = 128
WIDE = 2 * LANES
TERMS = 16
SPLITS = 3
RAW = 6
F32 = jnp.float32
BF16 = jnp.bfloat16


def up(n, m):
    return -(-n // m) * m


def split(value, parts):
    out = []
    for _ in range(parts):
        piece = value.astype(BF16).astype(F32)
        out.append(piece)
        value = value - piece
    return out


def spread():
    shape = (3 * TERMS, RAW)
    r, c = (lax.broadcasted_iota(jnp.int32, shape, d) for d in range(2))

    def steps(first, count):
        return sum(jnp.where(r >= first + 3 * (k + 1), 1, 0) for k in range(count))

    at = jnp.where(
        r < 15, 3 + r - 3 * steps(0, 4), jnp.where(
            (r >= 19) & (r < 28), steps(19, 2), jnp.where(
                (r >= 28) & (r < 31), r - 28, jnp.where(
                    (r >= 32) & (r < 35), r - 32, jnp.where((r >= 40) & (r < 43), r - 37, -1)))))
    return jnp.where(c == at, jnp.where((r >= 32) & (r < 35), -2.0, 1.0), 0.0).astype(BF16)


def features(rep, weight):
    lanes = rep.shape[1]
    row = lax.broadcasted_iota(jnp.int32, (8, lanes), 0)
    y2, g = rep[32:40], rep[40:48]
    norm = 0.25 * jnp.sum(y2 * y2, axis=0, keepdims=True)
    dot = -0.5 * weight * jnp.sum(y2 * g, axis=0, keepdims=True)
    m = split(norm + EPSILON2, 3)
    first = jnp.where((row >= 3) & (row < 6), 1.0, y2)
    first = jnp.where(row == 6, m[0], jnp.where(row == 7, m[1], first))
    second = jnp.where(row == 0, m[2], 0.0)
    near = jnp.concatenate([first, second], axis=0).astype(BF16)
    one = rep[0:8] * weight * jnp.where(row < 3, 1.0, rep[16:24])
    two = rep[8:16] * weight * jnp.where(row >= 4, norm, rep[24:32])
    two = two + jnp.where(row >= 4, dot * rep[24:32], 0.0)
    parts = split(jnp.concatenate([one, two], axis=0), SPLITS)
    return near, jnp.concatenate(parts, axis=0).astype(BF16)


def kernel(
    cfg,
    pair_target_far, pair_source_far, junction_cell_far, junction_target_far, wall_near_far,
    positions, density, upsample, quad_far, coarse_far, wall_points, wall_traction,
    out,
    pair_target, pair_source, junction_cell, junction_target, wall_near, quad, coarse,
    own, mine, cells, jsend, jrecv, wall_own, walls, ups, rows, quad_row, coarse_row, tail, xt, xs,
    local_sem, halo_send, halo_recv, junction_send, junction_recv, wall_send, wall_recv,
):
    count, points, fine_points, pairs, near, patch, segs, slabs, per_slab = cfg
    pt = xs.shape[2]
    rows_t = xt.shape[1]
    seg, slab = lax.axis_index("seg"), lax.axis_index("slab")

    barrier = pltpu.get_barrier_semaphore()
    for o in range(1, segs):
        pl.semaphore_signal(barrier, inc=1, device_id={"seg": lax.rem(seg + o, segs)}, device_id_type=MESH)
    for o in range(1, slabs):
        pl.semaphore_signal(barrier, inc=1, device_id={"slab": lax.rem(slab + o, slabs)}, device_id_type=MESH)

    copies = [
        pltpu.make_async_copy(positions.at[0], own.at[0], local_sem.at[0]),
        pltpu.make_async_copy(density.at[0], own.at[1], local_sem.at[1]),
        pltpu.make_async_copy(wall_points.at[0], wall_own.at[0], local_sem.at[2]),
        pltpu.make_async_copy(wall_traction.at[0], wall_own.at[1], local_sem.at[3]),
    ]
    big = pltpu.make_async_copy(upsample, ups, local_sem.at[4])
    tables = [
        pltpu.make_async_copy(source, target, local_sem.at[5 + i]) for i, (source, target) in enumerate([
            (pair_target_far, pair_target), (pair_source_far, pair_source), (junction_cell_far, junction_cell),
            (junction_target_far, junction_target), (wall_near_far, wall_near), (quad_far, quad), (coarse_far, coarse)])
    ]
    for copy in copies + tables:
        copy.start()
    big.start()
    for copy in copies + tables:
        copy.wait()

    mine[...] = jnp.zeros_like(mine)

    @pl.when(slab == 0)
    def _():
        cells[0:HALO] = jnp.zeros((HALO, RAW, pt), BF16)

    @pl.when(slab == slabs - 1)
    def _():
        cells[HALO + count:] = jnp.zeros((HALO, RAW, pt), BF16)

    coords = [own[0, i].astype(F32) for i in range(3)]
    loads = [own[1, i].astype(F32) for i in range(3)]
    for c in range(count):
        mine[c, :, 0:points] = jnp.concatenate(
            [line[c:c + 1] for line in coords + loads], axis=0).astype(BF16)
    cells[HALO:HALO + count] = mine[...]
    for b in range(segs):
        jsend[b] = mine[junction_cell[0, 0, b]]
    for p in range(per_slab):
        walls[slab * per_slab + p] = jnp.concatenate(
            [wall_own[0, p].astype(F32), wall_own[1, p].astype(F32)], axis=0).astype(BF16)
    pl.semaphore_wait(barrier, segs - 1 + slabs - 1)

    def halo_up():
        return pltpu.make_async_remote_copy(
            cells.at[pl.ds(count, HALO)], cells.at[pl.ds(0, HALO)], halo_send.at[0], halo_recv.at[0],
            device_id={"slab": lax.rem(slab + 1, slabs)}, device_id_type=MESH)

    def halo_down():
        return pltpu.make_async_remote_copy(
            cells.at[pl.ds(HALO, HALO)], cells.at[pl.ds(HALO + count, HALO)], halo_send.at[1], halo_recv.at[1],
            device_id={"slab": lax.rem(slab + slabs - 1, slabs)}, device_id_type=MESH)

    def junction(o):
        return pltpu.make_async_remote_copy(
            jsend.at[lax.rem(seg + o, segs)], jrecv.at[seg], junction_send.at[o], junction_recv.at[o],
            device_id={"seg": lax.rem(seg + o, segs)}, device_id_type=MESH)

    def junction_in(o):
        return pltpu.make_async_remote_copy(
            jsend.at[seg], jrecv.at[lax.rem(seg + segs - o, segs)], junction_send.at[o], junction_recv.at[o],
            device_id={"seg": lax.rem(seg + o, segs)}, device_id_type=MESH)

    def wall(o, of):
        slot = pl.ds(of * per_slab, per_slab)
        return pltpu.make_async_remote_copy(
            walls.at[slot], walls.at[slot], wall_send.at[o], wall_recv.at[o],
            device_id={"slab": lax.rem(slab + o, slabs)}, device_id_type=MESH)

    @pl.when(slab < slabs - 1)
    def _():
        halo_up().start()

    @pl.when(slab > 0)
    def _():
        halo_down().start()

    for o in range(1, segs):
        junction(o).start()
    for o in range(slabs - 1, 0, -1):
        wall(o, slab).start()

    chosen = spread()
    quad_row[...] = jnp.zeros_like(quad_row)
    coarse_row[...] = jnp.zeros_like(coarse_row)
    quad_row[:, 0:fine_points] = quad[...][None]
    coarse_row[:, 0:points] = coarse[...][None]
    tail[...] = jnp.zeros_like(tail)
    rows[...] = jnp.zeros_like(rows)
    xs[...] = jnp.zeros_like(xs)
    norms = split(coords[0] * coords[0] + coords[1] * coords[1] + coords[2] * coords[2], 3)
    rows[6:9] = jnp.ones((3, pt), F32)
    for c in range(count):
        for i in range(3):
            xs[c, i:i + 1, 0:points] = coords[i][c:c + 1]
            rows[i:i + 1, 0:points] = coords[i][c:c + 1]
            rows[3 + i:4 + i, 0:points] = norms[i][c:c + 1]
        xt[c] = rows[...].T[0:rows_t].astype(BF16)

    def repeat(raw):
        return jnp.dot(chosen, raw, preferred_element_type=F32)

    def distance(target, near_rows):
        return jnp.dot(xt[target], near_rows, preferred_element_type=F32)

    def weigh(value):
        inverse = lax.rsqrt(value)
        return (inverse * inverse * inverse).astype(BF16)

    def reduce(weights, value):
        sums = lax.dot_general(weights, value, (((1,), (1,)), ((), ())), preferred_element_type=F32)
        return sums[0:TERMS] + sums[TERMS:2 * TERMS] + sums[2 * TERMS:3 * TERMS]

    totals = {}

    def run(units):
        held = []
        for k in range(0, len(units) + 2, 2):
            fresh = []
            for item, target, make in units[k:k + 2]:
                near_rows, weights = features(*make())
                fresh.append((item, weights, distance(target, near_rows)))
            sums = [(item, reduce(weights, value)) for item, weights, value in held]
            held = [(item, weights, weigh(value)) for item, weights, value in fresh]
            for item, value in sums:
                totals[item] = totals[item] + value if item in totals else value

    @pl.when(slab > 0)
    def _():
        halo_up().wait_recv()

    @pl.when(slab < slabs - 1)
    def _():
        halo_down().wait_recv()

    big.wait()
    lhs = jnp.concatenate([repeat(cells[pair_source[0, k]]) for k in range(pairs)], axis=0)[:, 0:points].astype(BF16)

    def fine(start):
        stop = min(start + WIDE, fine_points)
        value = jnp.dot(lhs, ups[:, start:stop], preferred_element_type=F32)
        if stop - start < WIDE:
            tail[:, 0:stop - start] = value
            value = tail[:, 0:up(stop - start, LANES)]
        return value.astype(BF16).astype(F32)

    units = []
    for start in range(0, fine_points, WIDE):
        cache = []

        def make(k, start=start, cache=cache):
            if not cache:
                cache.append(fine(start))
            value = cache[0][3 * TERMS * k:3 * TERMS * (k + 1)]
            return value, quad_row[:, start:start + value.shape[1]]

        units += [(("pair", k), pair_target[0, k], functools.partial(make, k)) for k in range(pairs)]
    run(units)

    for o in range(1, segs):
        junction_in(o).wait_recv()
    units = []
    for start in range(0, pt, WIDE):
        for o in range(1, segs):
            def make(start=start, o=o):
                at = slice(start, min(start + WIDE, pt))
                return repeat(jrecv[lax.rem(seg + segs - o, segs), :, at]), coarse_row[:, at]

            units.append((("junction", o), junction_target[0, 0, lax.rem(seg + segs - o, segs)], make))
    run(units)

    for o in range(1, slabs):
        wall(o, lax.rem(slab + slabs - o, slabs)).wait_recv()
    units = []
    for c in range(count):
        def make(c=c):
            value = repeat(jnp.concatenate([walls[wall_near[0, n, c]] for n in range(near)], axis=1))
            return value, WALL_GAIN

        units.append((("wall", c), c, make))
    run(units)

    places = [(("pair", k), pair_target[0, k]) for k in range(pairs)]
    places += [(("junction", o), junction_target[0, 0, lax.rem(seg + segs - o, segs)]) for o in range(1, segs)]
    for c in range(count):
        total = totals["wall", c]
        for item, target in places:
            total = total + jnp.where(target == c, 1.0, 0.0) * totals[item]
        total = total[:, 0:points]
        x = xs[c, :, 0:points]
        x = [x[i:i + 1] for i in range(3)]
        a, b, h = total[0:3], [total[3 + 3 * i:6 + 3 * i] for i in range(3)], total[12:15]
        square = x[0] * x[0] + x[1] * x[1] + x[2] * x[2] + 2.0 * EPSILON2
        value = square * a + h - 2.0 * (x[0] * b[0] + x[1] * b[1] + x[2] * b[2])
        trace = b[0][0:1] + b[1][1:2] + b[2][2:3]
        lift = x[0] * a[0:1] + x[1] * a[1:2] + x[2] * a[2:3] - trace
        for i in range(3):
            along = x[0] * b[i][0:1] + x[1] * b[i][1:2] + x[2] * b[i][2:3]
            out[0, i, c:c + 1] = (value[i:i + 1] + x[i] * lift - along) * (1.0 / (8.0 * math.pi))

    @pl.when(slab < slabs - 1)
    def _():
        halo_up().wait_send()

    @pl.when(slab > 0)
    def _():
        halo_down().wait_send()

    for o in range(1, segs):
        junction(o).wait_send()
    for o in range(1, slabs):
        wall(o, slab).wait_send()


def local(segs, slabs, positions, density, upsample, quad_weights, coarse_weights, pair_target, pair_source,
          junction_cell, junction_target, wall_points, wall_traction, wall_near):
    count, points = positions.shape[1], positions.shape[3]
    turned = (1, 3, count, points)
    fine_points = upsample.shape[1]
    pairs, near = pair_target.shape[1], wall_near.shape[2]
    per_slab, patch = wall_points.shape[1], wall_points.shape[3]
    cfg = (count, points, fine_points, pairs, near, patch, segs, slabs, per_slab)
    pt = up(points, LANES)
    vmem = pl.BlockSpec(memory_space=pltpu.VMEM)
    far = pl.BlockSpec(memory_space=pl.ANY)
    dma = pltpu.SemaphoreType.DMA
    result = pl.pallas_call(
        functools.partial(kernel, cfg),
        out_shape=jax.ShapeDtypeStruct(turned, F32),
        in_specs=[far] * 12,
        out_specs=vmem,
        scratch_shapes=[
            pltpu.SMEM(pair_target.shape, jnp.int32),
            pltpu.SMEM(pair_source.shape, jnp.int32),
            pltpu.SMEM(junction_cell.shape, jnp.int32),
            pltpu.SMEM(junction_target.shape, jnp.int32),
            pltpu.SMEM((1, near, count), jnp.int32),
            pltpu.VMEM(quad_weights.shape, F32),
            pltpu.VMEM(coarse_weights.shape, F32),
            pltpu.VMEM((2,) + turned[1:], BF16),
            pltpu.VMEM((count, RAW, pt), BF16),
            pltpu.VMEM((count + 2 * HALO, RAW, pt), BF16),
            pltpu.VMEM((segs, RAW, pt), BF16),
            pltpu.VMEM((segs, RAW, pt), BF16),
            pltpu.VMEM((2, per_slab, 3, patch), BF16),
            pltpu.VMEM((slabs * per_slab, RAW, patch), BF16),
            pltpu.VMEM(upsample.shape, BF16),
            pltpu.VMEM((TERMS, pt), F32),
            pltpu.VMEM((1, up(fine_points, LANES)), F32),
            pltpu.VMEM((1, pt), F32),
            pltpu.VMEM((3 * TERMS * pairs, WIDE), F32),
            pltpu.VMEM((count, up(points, 16), TERMS), BF16),
            pltpu.VMEM((count, 3, pt), F32),
            dma((12,)), dma((2,)), dma((2,)), dma((segs,)), dma((segs,)), dma((slabs,)), dma((slabs,)),
        ],
        compiler_params=pltpu.CompilerParams(collective_id=0, has_side_effects=True),
    )(pair_target, pair_source, junction_cell, junction_target, wall_near.transpose(0, 2, 1),
      positions.transpose(0, 2, 1, 3), density.transpose(0, 2, 1, 3), upsample, quad_weights, coarse_weights,
      wall_points, wall_traction)
    return result.transpose(0, 2, 1, 3)


def solution(mesh):
    placed = (
        P("seg", "slab", None, None),
        P("seg", "slab", None, None),
        P(),
        P(),
        P(),
        P("seg", "slab"),
        P("seg", "slab"),
        P("seg", "slab", None),
        P("seg", "slab", None),
        P("seg", "slab", None, None),
        P("seg", "slab", None, None),
        P("seg", "slab", None),
    )
    body = functools.partial(local, mesh.shape["seg"], mesh.shape["slab"])
    return jax.shard_map(
        body, mesh=mesh, in_specs=placed, out_specs=P("seg", "slab", None, None), check_vma=False
    )
```

time: 23.5 us -> 19.3 us (0.82)
  Pallas kernels: 22 us -> 17.7 us
    pallas_call x1, Pallas kernels: 22 us -> 17.7 us  [local(): pl.pallas_call(functools.partial(kernel, cfg), out_shape=jax.ShapeDtypeSt...]
where the time goes in v1:
time: 19.3 us; the launch traced here: 19.1 us
  Pallas kernels  17.7 us (92%)
  local copies, waits for them, and re-layouts  1.39 us (7%)
    pallas_call x1, Pallas kernels, local(): pl.pallas_call(functools.partial(kernel, cfg), out_shape=jax.ShapeDtypeSt...  17.7 us
    unnamed x1, local copies, waits for them, and re-layouts  1.39 us

profile of v1, /device:TPU:1, one launch (start us, length us, event | category | flops | bytes accessed | tf_op | source)
XLA Modules:
  0.0 19.1 jit_solution(2621666165141293312)
XLA Ops:
  0.0 17.7 %shard_map.118 = f32[1,3,4,642]{3,2,1,0:T(4,128)} custom-call(s32[1,2]{1,0:T(1,128)} %pair_target_far.1, s32[1,2]{1,0:T(1,128)} %pair_source_far.1, s32[1,1,4]{2,1,0:T(1,128)} %junction_cell_far.1, s32[1,1,4]{2,1,0:T(1,128)} %junction_target_far.1, s32[1,2,4]{2,1,0:T(2,128)} %bitcast.7, bf16[1,3,4,642]{3,2,1,0:T(4,128)(2,1)} %bitcast.5, ...), custom_call_target="tpu_custom_call" | custom-call | tf_op jit(solution)/shard_map/pallas_call | solution.py:314
  17.7 1.4 %copy.14 = f32[1,4,3,642]{3,1,2,0:T(4,128)} copy(f32[1,4,3,642]{3,1,2,0:T(4,128)} %bitcast.4) | data formatting | bytes 61632

commit v2 on v1

--- a/solution.py
+++ b/solution.py
@@ -313,7 +313,7 @@
     dma = pltpu.SemaphoreType.DMA
     result = pl.pallas_call(
         functools.partial(kernel, cfg),
-        out_shape=jax.ShapeDtypeStruct(turned, F32),
+        out_shape=pltpu.VMEM(turned, F32),
         in_specs=[far] * 12,
         out_specs=vmem,
         scratch_shapes=[

time: 19.3 us -> 17.9 us (0.927)
  local copies, waits for them, and re-layouts: 1.39 us -> 0.62 us
  Pallas kernels: 17.7 us -> 17.1 us
    unnamed x1, local copies, waits for them, and re-layouts: 1.39 us -> 0.62 us
    pallas_call x1, Pallas kernels: 17.7 us -> 17.1 us  [local(): pl.pallas_call(functools.partial(kernel, cfg), out_shape=pltpu.VMEM(turne...]
where the time goes in v2:
time: 17.9 us; the launch traced here: 17.7 us
  Pallas kernels  17.1 us (96%)
  local copies, waits for them, and re-layouts  0.62 us (3%)
    pallas_call x1, Pallas kernels, local(): pl.pallas_call(functools.partial(kernel, cfg), out_shape=pltpu.VMEM(turne...  17.1 us
    unnamed x1, local copies, waits for them, and re-layouts  0.62 us

profile of v2, /device:TPU:1, one launch (start us, length us, event | category | flops | bytes accessed | tf_op | source)
XLA Modules:
  0.0 17.7 jit_solution(8437419127328913601)
XLA Ops:
  0.0 17.1 %shard_map.118 = f32[1,3,4,642]{3,2,1,0:T(4,128)S(1)} custom-call(s32[1,2]{1,0:T(1,128)} %pair_target_far.1, s32[1,2]{1,0:T(1,128)} %pair_source_far.1, s32[1,1,4]{2,1,0:T(1,128)} %junction_cell_far.1, s32[1,1,4]{2,1,0:T(1,128)} %junction_target_far.1, s32[1,2,4]{2,1,0:T(2,128)} %bitcast.7, bf16[1,3,4,642]{3,2,1,0:T(4,128)(2,1)} %bitcast.5, ...), custom_call_target="tpu_custom_call" | custom-call | tf_op jit(solution)/shard_map/pallas_call | solution.py:314
  17.1 0.6 %copy.14 = f32[1,4,3,642]{3,1,2,0:T(4,128)} copy(f32[1,4,3,642]{3,1,2,0:T(4,128)S(1)} %bitcast.4) | data formatting | bytes 61632

commit v3 on v2

--- a/solution.py
+++ b/solution.py
@@ -17,12 +17,20 @@
 TERMS = 16
 SPLITS = 3
 RAW = 6
+CORES = 2
+RELAY = 3
+RELAY_STEP = 4
 F32 = jnp.float32
 BF16 = jnp.bfloat16
 
 
 def up(n, m):
     return -(-n // m) * m
+
+
+def grid(n):
+    columns = max(k for k in range(1, n + 1) if n % k == 0 and k * k <= n)
+    return n // columns, columns
 
 
 def split(value, parts):
@@ -73,19 +81,52 @@
     positions, density, upsample, quad_far, coarse_far, wall_points, wall_traction,
     out,
     pair_target, pair_source, junction_cell, junction_target, wall_near, quad, coarse,
-    own, mine, cells, jsend, jrecv, wall_own, walls, ups, rows, quad_row, coarse_row, tail, xt, xs,
-    local_sem, halo_send, halo_recv, junction_send, junction_recv, wall_send, wall_recv,
+    own, mine, cells, jsend, mid, jrecv, wall_own, walls, ups, rows, quad_row, coarse_row, tail, xt, xs,
+    local_sem, halo_send, halo_recv, junction_send, junction_recv, wall_send, wall_recv, up_send, up_recv, down_send, down_recv,
 ):
     count, points, fine_points, pairs, near, patch, segs, slabs, per_slab = cfg
     pt = xs.shape[2]
     rows_t = xt.shape[1]
     seg, slab = lax.axis_index("seg"), lax.axis_index("slab")
+    lines, columns = grid(segs)
+    levels = slabs // CORES
+    line, column = lax.div(seg, columns), lax.rem(seg, columns)
+    level, core = lax.div(slab, CORES), lax.rem(slab, CORES)
+    partner = slab + 1 - 2 * core
+    above, below = level < levels - 1, level > 0
+
+    def turn(base, o, size):
+        return lax.rem(base + (o + size), size)
+
+    def across(dy, dx):
+        return {"seg": turn(line, dy, lines) * columns + turn(column, dx, columns)}
 
     barrier = pltpu.get_barrier_semaphore()
-    for o in range(1, segs):
-        pl.semaphore_signal(barrier, inc=1, device_id={"seg": lax.rem(seg + o, segs)}, device_id_type=MESH)
-    for o in range(1, slabs):
-        pl.semaphore_signal(barrier, inc=1, device_id={"slab": lax.rem(slab + o, slabs)}, device_id_type=MESH)
+
+    def greet(device):
+        pl.semaphore_signal(barrier, inc=1, device_id=device, device_id_type=MESH)
+
+    @pl.when(above)
+    def _():
+        greet({"slab": slab + CORES})
+
+    @pl.when(below)
+    def _():
+        greet({"slab": slab - CORES})
+
+    @pl.when((core == 1) & above)
+    def _():
+        greet({"slab": slab + 1})
+
+    @pl.when((core == 0) & below)
+    def _():
+        greet({"slab": slab - 1})
+
+    for dx in range(1, columns):
+        greet(across(0, dx))
+    for dy in range(1, lines):
+        greet(across(dy, 0))
+    greet({"slab": partner})
 
     copies = [
         pltpu.make_async_copy(positions.at[0], own.at[0], local_sem.at[0]),
@@ -122,11 +163,12 @@
             [line[c:c + 1] for line in coords + loads], axis=0).astype(BF16)
     cells[HALO:HALO + count] = mine[...]
     for b in range(segs):
-        jsend[b] = mine[junction_cell[0, 0, b]]
+        jsend[b % columns, b // columns] = mine[junction_cell[0, 0, b]]
     for p in range(per_slab):
         walls[slab * per_slab + p] = jnp.concatenate(
             [wall_own[0, p].astype(F32), wall_own[1, p].astype(F32)], axis=0).astype(BF16)
-    pl.semaphore_wait(barrier, segs - 1 + slabs - 1)
+    beside = jnp.where(above, 1, 0) + jnp.where(below, 1, 0) + jnp.where(core == 1, jnp.where(above, 1, 0), jnp.where(below, 1, 0))
+    pl.semaphore_wait(barrier, lines - 1 + columns - 1 + 1 + beside)
 
     def halo_up():
         return pltpu.make_async_remote_copy(
@@ -138,21 +180,69 @@
             cells.at[pl.ds(HALO, HALO)], cells.at[pl.ds(HALO + count, HALO)], halo_send.at[1], halo_recv.at[1],
             device_id={"slab": lax.rem(slab + slabs - 1, slabs)}, device_id_type=MESH)
 
-    def junction(o):
-        return pltpu.make_async_remote_copy(
-            jsend.at[lax.rem(seg + o, segs)], jrecv.at[seg], junction_send.at[o], junction_recv.at[o],
-            device_id={"seg": lax.rem(seg + o, segs)}, device_id_type=MESH)
-
-    def junction_in(o):
-        return pltpu.make_async_remote_copy(
-            jsend.at[seg], jrecv.at[lax.rem(seg + segs - o, segs)], junction_send.at[o], junction_recv.at[o],
-            device_id={"seg": lax.rem(seg + o, segs)}, device_id_type=MESH)
-
-    def wall(o, of):
+    def junction(dy, dx):
+        i = dy * columns + dx
+        sems = junction_send.at[i], junction_recv.at[i]
+        if dy == 0:
+            return pltpu.make_async_remote_copy(
+                jsend.at[turn(column, dx, columns)], mid.at[:, column], *sems,
+                device_id=across(0, dx), device_id_type=MESH)
+        if dx == 0:
+            return pltpu.make_async_remote_copy(
+                jsend.at[column, turn(line, dy, lines)], jrecv.at[line, column], *sems,
+                device_id=across(dy, 0), device_id_type=MESH)
+        came = turn(column, -dx, columns)
+        return pltpu.make_async_remote_copy(
+            mid.at[turn(line, dy, lines), came], jrecv.at[line, came], *sems,
+            device_id=across(dy, 0), device_id_type=MESH)
+
+    def junction_in(dy, dx):
+        i = dy * columns + dx
+        sems = junction_send.at[i], junction_recv.at[i]
+        came = turn(column, -dx, columns)
+        if dy == 0:
+            return pltpu.make_async_remote_copy(
+                jsend.at[0], mid.at[:, came], *sems, device_id=across(0, dx), device_id_type=MESH)
+        return pltpu.make_async_remote_copy(
+            jsend.at[0, 0], jrecv.at[turn(line, -dy, lines), came], *sems,
+            device_id=across(dy, 0), device_id_type=MESH)
+
+    steps = [(dy, dx) for dy in range(lines) for dx in range(columns) if dy + dx > 0]
+
+    def pass_junctions():
+        for dx in range(1, columns):
+            junction_in(0, dx).wait_recv()
+            for dy in range(1, lines):
+                junction(dy, dx).start()
+
+    def wall_swap(of):
         slot = pl.ds(of * per_slab, per_slab)
         return pltpu.make_async_remote_copy(
-            walls.at[slot], walls.at[slot], wall_send.at[o], wall_recv.at[o],
-            device_id={"slab": lax.rem(slab + o, slabs)}, device_id_type=MESH)
+            walls.at[slot], walls.at[slot], wall_send.at[0], wall_recv.at[0],
+            device_id={"slab": partner}, device_id_type=MESH)
+
+    def wall(t, way, of):
+        slot = pl.ds(of * (CORES * per_slab), CORES * per_slab)
+        send, recv = (up_send, up_recv) if way > 0 else (down_send, down_recv)
+        return pltpu.make_async_remote_copy(
+            walls.at[slot], walls.at[slot], send.at[t], recv.at[t],
+            device_id={"slab": slab + way * CORES}, device_id_type=MESH)
+
+    def wall_sends(t):
+        return [(above & (level >= t), wall(t, 1, level - t)), (below & (level + t < levels), wall(t, -1, level + t))]
+
+    def wall_arrivals(t):
+        return [(level > t, wall(t, 1, level - 1 - t)), (level + 1 + t < levels, wall(t, -1, level + 1 + t))]
+
+    def pass_walls(t):
+        if t == 0:
+            wall_swap(partner).wait_recv()
+        else:
+            for there, copy in wall_arrivals(t - 1):
+                pl.when(there)(copy.wait_recv)
+        if t < levels - 1:
+            for there, copy in wall_sends(t):
+                pl.when(there)(copy.start)
 
     @pl.when(slab < slabs - 1)
     def _():
@@ -162,10 +252,11 @@
     def _():
         halo_down().start()
 
-    for o in range(1, segs):
-        junction(o).start()
-    for o in range(slabs - 1, 0, -1):
-        wall(o, slab).start()
+    for dx in range(1, columns):
+        junction(0, dx).start()
+    for dy in range(1, lines):
+        junction(dy, 0).start()
+    wall_swap(slab).start()
 
     chosen = spread()
     quad_row[...] = jnp.zeros_like(quad_row)
@@ -199,10 +290,13 @@
         return sums[0:TERMS] + sums[TERMS:2 * TERMS] + sums[2 * TERMS:3 * TERMS]
 
     totals = {}
-
-    def run(units):
+    pass_walls(0)
+
+    def run(units, between={}):
         held = []
         for k in range(0, len(units) + 2, 2):
+            for act in between.get(k // 2, ()):
+                act()
             fresh = []
             for item, target, make in units[k:k + 2]:
                 near_rows, weights = features(*make())
@@ -242,22 +336,31 @@
             return value, quad_row[:, start:start + value.shape[1]]
 
         units += [(("pair", k), pair_target[0, k], functools.partial(make, k)) for k in range(pairs)]
-    run(units)
-
-    for o in range(1, segs):
-        junction_in(o).wait_recv()
+    between = {RELAY: [pass_junctions]}
+    for t in range(1, levels - 1):
+        between.setdefault(RELAY + RELAY_STEP * (t - 1), []).append(functools.partial(pass_walls, t))
+    end = len(units) // 2
+    run(units, {k: acts for k, acts in between.items() if k <= end})
+
+    for dy, dx in steps:
+        if dy > 0:
+            junction_in(dy, dx).wait_recv()
     units = []
     for start in range(0, pt, WIDE):
-        for o in range(1, segs):
-            def make(start=start, o=o):
+        for dy, dx in steps:
+            def make(start=start, dy=dy, dx=dx):
                 at = slice(start, min(start + WIDE, pt))
-                return repeat(jrecv[lax.rem(seg + segs - o, segs), :, at]), coarse_row[:, at]
-
-            units.append((("junction", o), junction_target[0, 0, lax.rem(seg + segs - o, segs)], make))
+                source = (mid if dy == 0 else jrecv)[turn(line, -dy, lines), turn(column, -dx, columns), :, at]
+                return repeat(source), coarse_row[:, at]
+
+            units.append((("junction", dy, dx), junction_target[0, 0, across(-dy, -dx)["seg"]], make))
     run(units)
 
-    for o in range(1, slabs):
-        wall(o, lax.rem(slab + slabs - o, slabs)).wait_recv()
+    for k in sorted(between):
+        if k > end:
+            for act in between[k]:
+                act()
+    pass_walls(levels - 1)
     units = []
     for c in range(count):
         def make(c=c):
@@ -268,7 +371,7 @@
     run(units)
 
     places = [(("pair", k), pair_target[0, k]) for k in range(pairs)]
-    places += [(("junction", o), junction_target[0, 0, lax.rem(seg + segs - o, segs)]) for o in range(1, segs)]
+    places += [(("junction", dy, dx), junction_target[0, 0, across(-dy, -dx)["seg"]]) for dy, dx in steps]
     for c in range(count):
         total = totals["wall", c]
         for item, target in places:
@@ -293,10 +396,12 @@
     def _():
         halo_down().wait_send()
 
-    for o in range(1, segs):
-        junction(o).wait_send()
-    for o in range(1, slabs):
-        wall(o, slab).wait_send()
+    for dy, dx in steps:
+        junction(dy, dx).wait_send()
+    wall_swap(slab).wait_send()
+    for t in range(levels - 1):
+        for there, copy in wall_sends(t):
+            pl.when(there)(copy.wait_send)
 
 
 def local(segs, slabs, positions, density, upsample, quad_weights, coarse_weights, pair_target, pair_source,
@@ -308,6 +413,8 @@
     per_slab, patch = wall_points.shape[1], wall_points.shape[3]
     cfg = (count, points, fine_points, pairs, near, patch, segs, slabs, per_slab)
     pt = up(points, LANES)
+    lines, columns = grid(segs)
+    levels = slabs // CORES
     vmem = pl.BlockSpec(memory_space=pltpu.VMEM)
     far = pl.BlockSpec(memory_space=pl.ANY)
     dma = pltpu.SemaphoreType.DMA
@@ -327,8 +434,9 @@
             pltpu.VMEM((2,) + turned[1:], BF16),
             pltpu.VMEM((count, RAW, pt), BF16),
             pltpu.VMEM((count + 2 * HALO, RAW, pt), BF16),
-            pltpu.VMEM((segs, RAW, pt), BF16),
-            pltpu.VMEM((segs, RAW, pt), BF16),
+            pltpu.VMEM((columns, lines, RAW, pt), BF16),
+            pltpu.VMEM((lines, columns, RAW, pt), BF16),
+            pltpu.VMEM((lines, columns, RAW, pt), BF16),
             pltpu.VMEM((2, per_slab, 3, patch), BF16),
             pltpu.VMEM((slabs * per_slab, RAW, patch), BF16),
             pltpu.VMEM(upsample.shape, BF16),
@@ -338,7 +446,8 @@
             pltpu.VMEM((3 * TERMS * pairs, WIDE), F32),
             pltpu.VMEM((count, up(points, 16), TERMS), BF16),
             pltpu.VMEM((count, 3, pt), F32),
-            dma((12,)), dma((2,)), dma((2,)), dma((segs,)), dma((segs,)), dma((slabs,)), dma((slabs,)),
+            dma((12,)), dma((2,)), dma((2,)), dma((segs,)), dma((segs,)), dma((1,)), dma((1,)),
+            dma((levels,)), dma((levels,)), dma((levels,)), dma((levels,)),
         ],
         compiler_params=pltpu.CompilerParams(collective_id=0, has_side_effects=True),
     )(pair_target, pair_source, junction_cell, junction_target, wall_near.transpose(0, 2, 1),

time: 17.9 us -> 17.2 us (0.961)
  the two profiles are of different devices: /device:TPU:1 before, /device:TPU:0 now
where the time goes in v3:
time: 17.2 us; the launch traced here: 17 us
  Pallas kernels  16.4 us (95%)
  local copies, waits for them, and re-layouts  0.62 us (4%)
    pallas_call x1, Pallas kernels, local(): pl.pallas_call(functools.partial(kernel, cfg), out_shape=pltpu.VMEM(turne...  16.4 us
    unnamed x1, local copies, waits for them, and re-layouts  0.62 us

profile of v3, /device:TPU:0, one launch (start us, length us, event | category | flops | bytes accessed | tf_op | source)
XLA Modules:
  0.0 17.0 jit_solution(10364832576750085593)
XLA Ops:
  0.0 16.4 %shard_map.118 = f32[1,3,4,642]{3,2,1,0:T(4,128)S(1)} custom-call(s32[1,2]{1,0:T(1,128)} %pair_target_far.1, s32[1,2]{1,0:T(1,128)} %pair_source_far.1, s32[1,1,4]{2,1,0:T(1,128)} %junction_cell_far.1, s32[1,1,4]{2,1,0:T(1,128)} %junction_target_far.1, s32[1,2,4]{2,1,0:T(2,128)} %bitcast.7, bf16[1,3,4,642]{3,2,1,0:T(4,128)(2,1)} %bitcast.5, ...), custom_call_target="tpu_custom_call" | custom-call | tf_op jit(solution)/shard_map/pallas_call | solution.py:421
  16.4 0.6 %copy.14 = f32[1,4,3,642]{3,1,2,0:T(4,128)} copy(f32[1,4,3,642]{3,1,2,0:T(4,128)S(1)} %bitcast.4) | data formatting | bytes 61632

commit v4 on v3

--- a/solution.py
+++ b/solution.py
@@ -17,6 +17,7 @@
 TERMS = 16
 SPLITS = 3
 RAW = 6
+PART = 3 * WIDE
 CORES = 2
 RELAY = 3
 RELAY_STEP = 4
@@ -81,8 +82,8 @@
     positions, density, upsample, quad_far, coarse_far, wall_points, wall_traction,
     out,
     pair_target, pair_source, junction_cell, junction_target, wall_near, quad, coarse,
-    own, mine, cells, jsend, mid, jrecv, wall_own, walls, ups, rows, quad_row, coarse_row, tail, xt, xs,
-    local_sem, halo_send, halo_recv, junction_send, junction_recv, wall_send, wall_recv, up_send, up_recv, down_send, down_recv,
+    own, mine, jsend, mid, jrecv, wall_own, walls, ups, rows, quad_row, coarse_row, xt, xs, held,
+    local_sem, halo_send, halo_recv, junction_send, junction_recv, wall_send, wall_recv, up_send, up_recv, down_send, down_recv, *fine,
 ):
     count, points, fine_points, pairs, near, patch, segs, slabs, per_slab = cfg
     pt = xs.shape[2]
@@ -148,36 +149,65 @@
 
     mine[...] = jnp.zeros_like(mine)
 
-    @pl.when(slab == 0)
-    def _():
-        cells[0:HALO] = jnp.zeros((HALO, RAW, pt), BF16)
-
-    @pl.when(slab == slabs - 1)
-    def _():
-        cells[HALO + count:] = jnp.zeros((HALO, RAW, pt), BF16)
+    parts = [(start, part.shape[2]) for start, part in zip(range(0, up(fine_points, LANES), PART), fine)]
+    for part in fine:
+        @pl.when(slab == 0)
+        def _():
+            part[0:HALO] = jnp.zeros((HALO,) + part.shape[1:], BF16)
+
+        @pl.when(slab == slabs - 1)
+        def _():
+            part[HALO + count:] = jnp.zeros((HALO,) + part.shape[1:], BF16)
 
     coords = [own[0, i].astype(F32) for i in range(3)]
     loads = [own[1, i].astype(F32) for i in range(3)]
+    rest = jnp.zeros((8 - RAW, points), F32)
+    raws = [jnp.concatenate([line[c:c + 1] for line in coords + loads] + [rest], axis=0) for c in range(count)]
     for c in range(count):
-        mine[c, :, 0:points] = jnp.concatenate(
-            [line[c:c + 1] for line in coords + loads], axis=0).astype(BF16)
-    cells[HALO:HALO + count] = mine[...]
+        mine[c, :, 0:points] = raws[c][0:RAW].astype(BF16)
+    lhs = jnp.concatenate(raws, axis=0).astype(BF16)
     for b in range(segs):
         jsend[b % columns, b // columns] = mine[junction_cell[0, 0, b]]
     for p in range(per_slab):
         walls[slab * per_slab + p] = jnp.concatenate(
             [wall_own[0, p].astype(F32), wall_own[1, p].astype(F32)], axis=0).astype(BF16)
+    chosen = spread()
+    quad_row[...] = jnp.zeros_like(quad_row)
+    coarse_row[...] = jnp.zeros_like(coarse_row)
+    quad_row[:, 0:fine_points] = quad[...][None]
+    coarse_row[:, 0:points] = coarse[...][None]
+    rows[...] = jnp.zeros_like(rows)
+    xs[...] = jnp.zeros_like(xs)
+    norms = split(coords[0] * coords[0] + coords[1] * coords[1] + coords[2] * coords[2], 3)
+    rows[6:9] = jnp.ones((3, pt), F32)
+    for c in range(count):
+        for i in range(3):
+            xs[c, i:i + 1, 0:points] = coords[i][c:c + 1]
+            rows[i:i + 1, 0:points] = coords[i][c:c + 1]
+            rows[3 + i:4 + i, 0:points] = norms[i][c:c + 1]
+        xt[c] = rows[...].T[0:rows_t].astype(BF16)
+
+    big.wait()
+    for (start, size), part in zip(parts, fine):
+        for at in range(0, size, WIDE):
+            stop = min(start + at + WIDE, fine_points)
+            value = jnp.dot(lhs, ups[:, start + at:stop], preferred_element_type=F32)
+            width = min(WIDE, size - at)
+            if stop - start - at < width:
+                value = jnp.concatenate([value, jnp.zeros((8 * count, width - value.shape[1]), F32)], axis=1)
+            for c in range(count):
+                part[HALO + c, :, at:at + width] = value[8 * c:8 * c + RAW].astype(BF16)
     beside = jnp.where(above, 1, 0) + jnp.where(below, 1, 0) + jnp.where(core == 1, jnp.where(above, 1, 0), jnp.where(below, 1, 0))
     pl.semaphore_wait(barrier, lines - 1 + columns - 1 + 1 + beside)
 
-    def halo_up():
-        return pltpu.make_async_remote_copy(
-            cells.at[pl.ds(count, HALO)], cells.at[pl.ds(0, HALO)], halo_send.at[0], halo_recv.at[0],
+    def halo_up(p):
+        return pltpu.make_async_remote_copy(
+            fine[p].at[pl.ds(count, HALO)], fine[p].at[pl.ds(0, HALO)], halo_send.at[0, p], halo_recv.at[0, p],
             device_id={"slab": lax.rem(slab + 1, slabs)}, device_id_type=MESH)
 
-    def halo_down():
-        return pltpu.make_async_remote_copy(
-            cells.at[pl.ds(HALO, HALO)], cells.at[pl.ds(HALO + count, HALO)], halo_send.at[1], halo_recv.at[1],
+    def halo_down(p):
+        return pltpu.make_async_remote_copy(
+            fine[p].at[pl.ds(HALO, HALO)], fine[p].at[pl.ds(HALO + count, HALO)], halo_send.at[1, p], halo_recv.at[1, p],
             device_id={"slab": lax.rem(slab + slabs - 1, slabs)}, device_id_type=MESH)
 
     def junction(dy, dx):
@@ -244,37 +274,15 @@
             for there, copy in wall_sends(t):
                 pl.when(there)(copy.start)
 
-    @pl.when(slab < slabs - 1)
-    def _():
-        halo_up().start()
-
-    @pl.when(slab > 0)
-    def _():
-        halo_down().start()
-
+    for p in range(len(fine)):
+        pl.when(slab < slabs - 1)(halo_up(p).start)
+        pl.when(slab > 0)(halo_down(p).start)
     for dx in range(1, columns):
         junction(0, dx).start()
     for dy in range(1, lines):
         junction(dy, 0).start()
     wall_swap(slab).start()
 
-    chosen = spread()
-    quad_row[...] = jnp.zeros_like(quad_row)
-    coarse_row[...] = jnp.zeros_like(coarse_row)
-    quad_row[:, 0:fine_points] = quad[...][None]
-    coarse_row[:, 0:points] = coarse[...][None]
-    tail[...] = jnp.zeros_like(tail)
-    rows[...] = jnp.zeros_like(rows)
-    xs[...] = jnp.zeros_like(xs)
-    norms = split(coords[0] * coords[0] + coords[1] * coords[1] + coords[2] * coords[2], 3)
-    rows[6:9] = jnp.ones((3, pt), F32)
-    for c in range(count):
-        for i in range(3):
-            xs[c, i:i + 1, 0:points] = coords[i][c:c + 1]
-            rows[i:i + 1, 0:points] = coords[i][c:c + 1]
-            rows[3 + i:4 + i, 0:points] = norms[i][c:c + 1]
-        xt[c] = rows[...].T[0:rows_t].astype(BF16)
-
     def repeat(raw):
         return jnp.dot(chosen, raw, preferred_element_type=F32)
 
@@ -293,50 +301,36 @@
     pass_walls(0)
 
     def run(units, between={}):
-        held = []
+        before = []
         for k in range(0, len(units) + 2, 2):
             for act in between.get(k // 2, ()):
                 act()
             fresh = []
-            for item, target, make in units[k:k + 2]:
+            for u, (item, target, make) in enumerate(units[k:k + 2]):
                 near_rows, weights = features(*make())
-                fresh.append((item, weights, distance(target, near_rows)))
-            sums = [(item, reduce(weights, value)) for item, weights, value in held]
-            held = [(item, weights, weigh(value)) for item, weights, value in fresh]
-            for item, value in sums:
+                at = held.at[k // 2 % 2, u, :, 0:near_rows.shape[1]]
+                at[...] = weigh(distance(target, near_rows))
+                fresh.append((item, weights, at))
+            for item, weights, at in before:
+                value = reduce(weights, at[...])
                 totals[item] = totals[item] + value if item in totals else value
-
-    @pl.when(slab > 0)
-    def _():
-        halo_up().wait_recv()
-
-    @pl.when(slab < slabs - 1)
-    def _():
-        halo_down().wait_recv()
-
-    big.wait()
-    lhs = jnp.concatenate([repeat(cells[pair_source[0, k]]) for k in range(pairs)], axis=0)[:, 0:points].astype(BF16)
-
-    def fine(start):
-        stop = min(start + WIDE, fine_points)
-        value = jnp.dot(lhs, ups[:, start:stop], preferred_element_type=F32)
-        if stop - start < WIDE:
-            tail[:, 0:stop - start] = value
-            value = tail[:, 0:up(stop - start, LANES)]
-        return value.astype(BF16).astype(F32)
-
+            before = fresh
+
+    def arrive(p):
+        pl.when(slab > 0)(halo_up(p).wait_recv)
+        pl.when(slab < slabs - 1)(halo_down(p).wait_recv)
+
+    between = {}
     units = []
-    for start in range(0, fine_points, WIDE):
-        cache = []
-
-        def make(k, start=start, cache=cache):
-            if not cache:
-                cache.append(fine(start))
-            value = cache[0][3 * TERMS * k:3 * TERMS * (k + 1)]
-            return value, quad_row[:, start:start + value.shape[1]]
-
-        units += [(("pair", k), pair_target[0, k], functools.partial(make, k)) for k in range(pairs)]
-    between = {RELAY: [pass_junctions]}
+    for p, (start, size) in enumerate(parts):
+        between[len(units) // pairs * pairs // 2] = [functools.partial(arrive, p)]
+        for at in range(0, size, WIDE):
+            for k in range(pairs):
+                def make(k=k, p=p, at=at, start=start, stop=min(at + WIDE, size)):
+                    return repeat(fine[p][pair_source[0, k], :, at:stop]), quad_row[:, start + at:start + stop]
+
+                units.append((("pair", k), pair_target[0, k], make))
+    between.setdefault(RELAY, []).append(pass_junctions)
     for t in range(1, levels - 1):
         between.setdefault(RELAY + RELAY_STEP * (t - 1), []).append(functools.partial(pass_walls, t))
     end = len(units) // 2
@@ -388,14 +382,9 @@
             along = x[0] * b[i][0:1] + x[1] * b[i][1:2] + x[2] * b[i][2:3]
             out[0, i, c:c + 1] = (value[i:i + 1] + x[i] * lift - along) * (1.0 / (8.0 * math.pi))
 
-    @pl.when(slab < slabs - 1)
-    def _():
-        halo_up().wait_send()
-
-    @pl.when(slab > 0)
-    def _():
-        halo_down().wait_send()
-
+    for p in range(len(fine)):
+        pl.when(slab < slabs - 1)(halo_up(p).wait_send)
+        pl.when(slab > 0)(halo_down(p).wait_send)
     for dy, dx in steps:
         junction(dy, dx).wait_send()
     wall_swap(slab).wait_send()
@@ -415,6 +404,7 @@
     pt = up(points, LANES)
     lines, columns = grid(segs)
     levels = slabs // CORES
+    widths = [min(PART, up(fine_points, LANES) - start) for start in range(0, up(fine_points, LANES), PART)]
     vmem = pl.BlockSpec(memory_space=pltpu.VMEM)
     far = pl.BlockSpec(memory_space=pl.ANY)
     dma = pltpu.SemaphoreType.DMA
@@ -433,7 +423,6 @@
             pltpu.VMEM(coarse_weights.shape, F32),
             pltpu.VMEM((2,) + turned[1:], BF16),
             pltpu.VMEM((count, RAW, pt), BF16),
-            pltpu.VMEM((count + 2 * HALO, RAW, pt), BF16),
             pltpu.VMEM((columns, lines, RAW, pt), BF16),
             pltpu.VMEM((lines, columns, RAW, pt), BF16),
             pltpu.VMEM((lines, columns, RAW, pt), BF16),
@@ -443,11 +432,12 @@
             pltpu.VMEM((TERMS, pt), F32),
             pltpu.VMEM((1, up(fine_points, LANES)), F32),
             pltpu.VMEM((1, pt), F32),
-            pltpu.VMEM((3 * TERMS * pairs, WIDE), F32),
             pltpu.VMEM((count, up(points, 16), TERMS), BF16),
             pltpu.VMEM((count, 3, pt), F32),
-            dma((12,)), dma((2,)), dma((2,)), dma((segs,)), dma((segs,)), dma((1,)), dma((1,)),
+            pltpu.VMEM((2, 2, up(points, 16), WIDE), BF16),
+            dma((12,)), dma((2, len(widths))), dma((2, len(widths))), dma((segs,)), dma((segs,)), dma((1,)), dma((1,)),
             dma((levels,)), dma((levels,)), dma((levels,)), dma((levels,)),
+            *[pltpu.VMEM((count + 2 * HALO, RAW, width), BF16) for width in widths],
         ],
         compiler_params=pltpu.CompilerParams(collective_id=0, has_side_effects=True),
     )(pair_target, pair_source, junction_cell, junction_target, wall_near.transpose(0, 2, 1),

time: 17.2 us -> 18.3 us (1.064)
  Pallas kernels: 16.4 us -> 17.6 us
    pallas_call x1, Pallas kernels: 16.4 us -> 17.6 us  [local(): pl.pallas_call(functools.partial(kernel, cfg), out_shape=pltpu.VMEM(turne...]
where the time goes in v4:
time: 18.3 us; the launch traced here: 18.2 us
  Pallas kernels  17.6 us (96%)
  local copies, waits for them, and re-layouts  0.62 us (3%)
    pallas_call x1, Pallas kernels, local(): pl.pallas_call(functools.partial(kernel, cfg), out_shape=pltpu.VMEM(turne...  17.6 us
    unnamed x1, local copies, waits for them, and re-layouts  0.62 us

profile of v4, /device:TPU:0, one launch (start us, length us, event | category | flops | bytes accessed | tf_op | source)
XLA Modules:
  0.0 18.2 jit_solution(13677632152273465962)
XLA Ops:
  0.0 17.6 %shard_map.118 = f32[1,3,4,642]{3,2,1,0:T(4,128)S(1)} custom-call(s32[1,2]{1,0:T(1,128)} %pair_target_far.1, s32[1,2]{1,0:T(1,128)} %pair_source_far.1, s32[1,1,4]{2,1,0:T(1,128)} %junction_cell_far.1, s32[1,1,4]{2,1,0:T(1,128)} %junction_target_far.1, s32[1,2,4]{2,1,0:T(2,128)} %bitcast.7, bf16[1,3,4,642]{3,2,1,0:T(4,128)(2,1)} %bitcast.5, ...), custom_call_target="tpu_custom_call" | custom-call | tf_op jit(solution)/shard_map/pallas_call | solution.py:411
  17.6 0.6 %copy.14 = f32[1,4,3,642]{3,1,2,0:T(4,128)} copy(f32[1,4,3,642]{3,1,2,0:T(4,128)S(1)} %bitcast.4) | data formatting | bytes 61632

commit v5 on v4

--- a/solution.py
+++ b/solution.py
@@ -17,7 +17,7 @@
 TERMS = 16
 SPLITS = 3
 RAW = 6
-PART = 3 * WIDE
+PARTS = (2 * WIDE, 4 * WIDE)
 CORES = 2
 RELAY = 3
 RELAY_STEP = 4
@@ -27,6 +27,15 @@
 
 def up(n, m):
     return -(-n // m) * m
+
+
+def cuts(n):
+    out, start, stop = [], 0, up(n, LANES)
+    for width in PARTS + (stop,):
+        if start < stop:
+            out.append((start, min(width, stop - start)))
+            start += out[-1][1]
+    return out
 
 
 def grid(n):
@@ -82,11 +91,11 @@
     positions, density, upsample, quad_far, coarse_far, wall_points, wall_traction,
     out,
     pair_target, pair_source, junction_cell, junction_target, wall_near, quad, coarse,
-    own, mine, jsend, mid, jrecv, wall_own, walls, ups, rows, quad_row, coarse_row, xt, xs, held,
+    own, mine, jsend, mid, jrecv, wall_own, walls, ups, rows, quad_row, coarse_row, xt, xs, held, nears, weights,
     local_sem, halo_send, halo_recv, junction_send, junction_recv, wall_send, wall_recv, up_send, up_recv, down_send, down_recv, *fine,
 ):
     count, points, fine_points, pairs, near, patch, segs, slabs, per_slab = cfg
-    pt = xs.shape[2]
+    pt, qp = xs.shape[2], quad_row.shape[1]
     rows_t = xt.shape[1]
     seg, slab = lax.axis_index("seg"), lax.axis_index("slab")
     lines, columns = grid(segs)
@@ -149,7 +158,7 @@
 
     mine[...] = jnp.zeros_like(mine)
 
-    parts = [(start, part.shape[2]) for start, part in zip(range(0, up(fine_points, LANES), PART), fine)]
+    parts = cuts(fine_points)
     for part in fine:
         @pl.when(slab == 0)
         def _():
@@ -300,69 +309,98 @@
     totals = {}
     pass_walls(0)
 
-    def run(units, between={}):
+    def run(units, between):
         before = []
         for k in range(0, len(units) + 2, 2):
             for act in between.get(k // 2, ()):
                 act()
             fresh = []
-            for u, (item, target, make) in enumerate(units[k:k + 2]):
-                near_rows, weights = features(*make())
-                at = held.at[k // 2 % 2, u, :, 0:near_rows.shape[1]]
-                at[...] = weigh(distance(target, near_rows))
-                fresh.append((item, weights, at))
-            for item, weights, at in before:
-                value = reduce(weights, at[...])
+            for u, (item, target, start, size) in enumerate(units[k:k + 2]):
+                at = held.at[k // 2 % 2, u, :, 0:size]
+                at[...] = weigh(distance(target, nears[:, start:start + size]))
+                fresh.append((item, start, size, at))
+            for item, start, size, at in before:
+                value = reduce(weights[:, start:start + size], at[...])
                 totals[item] = totals[item] + value if item in totals else value
             before = fresh
+
+    def prepare(start, rep, weight):
+        at = slice(start, start + rep.shape[1])
+        nears[:, at], weights[:, at] = features(rep, weight)
 
     def arrive(p):
         pl.when(slab > 0)(halo_up(p).wait_recv)
         pl.when(slab < slabs - 1)(halo_down(p).wait_recv)
 
+    def prepare_pairs(p):
+        start, size = parts[p]
+        for k in range(pairs):
+            prepare(k * qp + start, repeat(fine[p][pair_source[0, k]]), quad_row[:, start:start + size])
+
+    def prepare_junction(i, dy, dx):
+        source = (mid if dy == 0 else jrecv)[turn(line, -dy, lines), turn(column, -dx, columns)]
+        prepare(pairs * qp + i * pt, repeat(source), coarse_row[...])
+
+    def prepare_walls():
+        near_by = jnp.concatenate([walls[wall_near[0, n, c]] for c in range(count) for n in range(near)], axis=1)
+        prepare(pairs * qp + len(steps) * pt, repeat(near_by), WALL_GAIN)
+
+    steps = sorted(steps, key=lambda step: min(step) > 0)
+    direct = [i for i, step in enumerate(steps) if min(step) == 0]
+    relayed = [i for i, step in enumerate(steps) if min(step) > 0]
+
+    def arrive_junctions(which):
+        for i in which:
+            if steps[i][0] > 0:
+                junction_in(*steps[i]).wait_recv()
+        for i in which:
+            prepare_junction(i, *steps[i])
+
+    units = []
+    firsts = []
+    for start, size in parts:
+        firsts.append(len(units) // 2)
+        for at in range(start, start + size, WIDE):
+            units += [(("pair", k), pair_target[0, k], k * qp + at, min(WIDE, start + size - at)) for k in range(pairs)]
+
+    def junction_units(which):
+        return [
+            (("junction",) + steps[i], junction_target[0, 0, across(-steps[i][0], -steps[i][1])["seg"]],
+             pairs * qp + i * pt + at, min(WIDE, pt - at)) for at in range(0, pt, WIDE) for i in which]
+
+    ends = [len(units) // 2]
+    units += junction_units(direct)
+    ends.append(len(units) // 2)
+    units += junction_units(relayed)
+    ends.append(len(units) // 2)
+    base = pairs * qp + len(steps) * pt
+    span = near * up(patch, LANES)
+    for c in range(count):
+        units += [(("wall", c), c, base + c * span + at, min(WIDE, span - at)) for at in range(0, span, WIDE)]
+
     between = {}
-    units = []
-    for p, (start, size) in enumerate(parts):
-        between[len(units) // pairs * pairs // 2] = [functools.partial(arrive, p)]
-        for at in range(0, size, WIDE):
-            for k in range(pairs):
-                def make(k=k, p=p, at=at, start=start, stop=min(at + WIDE, size)):
-                    return repeat(fine[p][pair_source[0, k], :, at:stop]), quad_row[:, start + at:start + stop]
-
-                units.append((("pair", k), pair_target[0, k], make))
-    between.setdefault(RELAY, []).append(pass_junctions)
-    for t in range(1, levels - 1):
-        between.setdefault(RELAY + RELAY_STEP * (t - 1), []).append(functools.partial(pass_walls, t))
-    end = len(units) // 2
-    run(units, {k: acts for k, acts in between.items() if k <= end})
-
-    for dy, dx in steps:
-        if dy > 0:
-            junction_in(dy, dx).wait_recv()
-    units = []
-    for start in range(0, pt, WIDE):
-        for dy, dx in steps:
-            def make(start=start, dy=dy, dx=dx):
-                at = slice(start, min(start + WIDE, pt))
-                source = (mid if dy == 0 else jrecv)[turn(line, -dy, lines), turn(column, -dx, columns), :, at]
-                return repeat(source), coarse_row[:, at]
-
-            units.append((("junction", dy, dx), junction_target[0, 0, across(-dy, -dx)["seg"]], make))
-    run(units)
-
-    for k in sorted(between):
-        if k > end:
-            for act in between[k]:
-                act()
-    pass_walls(levels - 1)
-    units = []
-    for c in range(count):
-        def make(c=c):
-            value = repeat(jnp.concatenate([walls[wall_near[0, n, c]] for n in range(near)], axis=1))
-            return value, WALL_GAIN
-
-        units.append((("wall", c), c, make))
-    run(units)
+
+    def when(k, *acts):
+        between.setdefault(k, []).extend(acts)
+
+    last = len(parts) - 1
+    when(0, *[functools.partial(f, 0) for f in (arrive, prepare_pairs)])
+    for p in range(1, len(parts)):
+        when(firsts[p - 1], functools.partial(arrive, p))
+        if p == min(2, last):
+            when(firsts[p - 1], pass_junctions)
+        if 1 < p <= levels - 1:
+            when(firsts[p - 1], functools.partial(pass_walls, p - 1))
+        when(firsts[p - 1], functools.partial(prepare_pairs, p))
+    done = max(last - 1, 0)
+    if last == 0:
+        when(0, pass_junctions)
+    when(firsts[last], functools.partial(arrive_junctions, direct))
+    if done + 1 < levels:
+        when(firsts[last], functools.partial(pass_walls, done + 1))
+    when(ends[0], functools.partial(arrive_junctions, relayed))
+    when(ends[1], *[functools.partial(pass_walls, t) for t in range(done + 2, levels)], prepare_walls)
+    run(units, between)
 
     places = [(("pair", k), pair_target[0, k]) for k in range(pairs)]
     places += [(("junction", dy, dx), junction_target[0, 0, across(-dy, -dx)["seg"]]) for dy, dx in steps]
@@ -404,7 +442,8 @@
     pt = up(points, LANES)
     lines, columns = grid(segs)
     levels = slabs // CORES
-    widths = [min(PART, up(fine_points, LANES) - start) for start in range(0, up(fine_points, LANES), PART)]
+    widths = [width for _, width in cuts(fine_points)]
+    lanes = pairs * up(fine_points, LANES) + (segs - 1) * pt + count * near * up(patch, LANES)
     vmem = pl.BlockSpec(memory_space=pltpu.VMEM)
     far = pl.BlockSpec(memory_space=pl.ANY)
     dma = pltpu.SemaphoreType.DMA
@@ -435,6 +474,8 @@
             pltpu.VMEM((count, up(points, 16), TERMS), BF16),
             pltpu.VMEM((count, 3, pt), F32),
             pltpu.VMEM((2, 2, up(points, 16), WIDE), BF16),
+            pltpu.VMEM((TERMS, lanes), BF16),
+            pltpu.VMEM((SPLITS * TERMS, lanes), BF16),
             dma((12,)), dma((2, len(widths))), dma((2, len(widths))), dma((segs,)), dma((segs,)), dma((1,)), dma((1,)),
             dma((levels,)), dma((levels,)), dma((levels,)), dma((levels,)),
             *[pltpu.VMEM((count + 2 * HALO, RAW, width), BF16) for width in widths],

time: 18.3 us -> 17.4 us (0.951)
  Pallas kernels: 17.6 us -> 16.7 us
    pallas_call x1, Pallas kernels: 17.6 us -> 16.7 us  [local(): pl.pallas_call(functools.partial(kernel, cfg), out_shape=pltpu.VMEM(turne...]
where the time goes in v5:
time: 17.4 us; the launch traced here: 17.3 us
  Pallas kernels  16.7 us (96%)
  local copies, waits for them, and re-layouts  0.62 us (4%)
    pallas_call x1, Pallas kernels, local(): pl.pallas_call(functools.partial(kernel, cfg), out_shape=pltpu.VMEM(turne...  16.7 us
    unnamed x1, local copies, waits for them, and re-layouts  0.62 us

profile of v5, /device:TPU:0, one launch (start us, length us, event | category | flops | bytes accessed | tf_op | source)
XLA Modules:
  0.0 17.3 jit_solution(7088753584341078445)
XLA Ops:
  0.0 16.7 %shard_map.118 = f32[1,3,4,642]{3,2,1,0:T(4,128)S(1)} custom-call(s32[1,2]{1,0:T(1,128)} %pair_target_far.1, s32[1,2]{1,0:T(1,128)} %pair_source_far.1, s32[1,1,4]{2,1,0:T(1,128)} %junction_cell_far.1, s32[1,1,4]{2,1,0:T(1,128)} %junction_target_far.1, s32[1,2,4]{2,1,0:T(2,128)} %bitcast.7, bf16[1,3,4,642]{3,2,1,0:T(4,128)(2,1)} %bitcast.5, ...), custom_call_target="tpu_custom_call" | custom-call | tf_op jit(solution)/shard_map/pallas_call | solution.py:450
  16.7 0.6 %copy.14 = f32[1,4,3,642]{3,1,2,0:T(4,128)} copy(f32[1,4,3,642]{3,1,2,0:T(4,128)S(1)} %bitcast.4) | data formatting | bytes 61632

commit v6 on v5

--- a/solution.py
+++ b/solution.py
@@ -91,8 +91,8 @@
     positions, density, upsample, quad_far, coarse_far, wall_points, wall_traction,
     out,
     pair_target, pair_source, junction_cell, junction_target, wall_near, quad, coarse,
-    own, mine, jsend, mid, jrecv, wall_own, walls, ups, rows, quad_row, coarse_row, xt, xs, held, nears, weights,
-    local_sem, halo_send, halo_recv, junction_send, junction_recv, wall_send, wall_recv, up_send, up_recv, down_send, down_recv, *fine,
+    own, mine, jsend, jrecv, wall_own, walls, ups, rows, quad_row, coarse_row, xt, xs, held, nears, weights,
+    local_sem, halo_send, halo_recv, junction_send, junction_recv, wall_send, wall_recv, column_in, above_in, below_in, *fine,
 ):
     count, points, fine_points, pairs, near, patch, segs, slabs, per_slab = cfg
     pt, qp = xs.shape[2], quad_row.shape[1]
@@ -119,18 +119,12 @@
     @pl.when(above)
     def _():
         greet({"slab": slab + CORES})
+        greet({"slab": partner + CORES})
 
     @pl.when(below)
     def _():
         greet({"slab": slab - CORES})
-
-    @pl.when((core == 1) & above)
-    def _():
-        greet({"slab": slab + 1})
-
-    @pl.when((core == 0) & below)
-    def _():
-        greet({"slab": slab - 1})
+        greet({"slab": partner - CORES})
 
     for dx in range(1, columns):
         greet(across(0, dx))
@@ -176,7 +170,7 @@
         mine[c, :, 0:points] = raws[c][0:RAW].astype(BF16)
     lhs = jnp.concatenate(raws, axis=0).astype(BF16)
     for b in range(segs):
-        jsend[b % columns, b // columns] = mine[junction_cell[0, 0, b]]
+        jsend[b] = mine[junction_cell[0, 0, b]]
     for p in range(per_slab):
         walls[slab * per_slab + p] = jnp.concatenate(
             [wall_own[0, p].astype(F32), wall_own[1, p].astype(F32)], axis=0).astype(BF16)
@@ -196,8 +190,8 @@
             rows[3 + i:4 + i, 0:points] = norms[i][c:c + 1]
         xt[c] = rows[...].T[0:rows_t].astype(BF16)
 
-    big.wait()
-    for (start, size), part in zip(parts, fine):
+    def refine(p):
+        (start, size), part = parts[p], fine[p]
         for at in range(0, size, WIDE):
             stop = min(start + at + WIDE, fine_points)
             value = jnp.dot(lhs, ups[:, start + at:stop], preferred_element_type=F32)
@@ -206,8 +200,11 @@
                 value = jnp.concatenate([value, jnp.zeros((8 * count, width - value.shape[1]), F32)], axis=1)
             for c in range(count):
                 part[HALO + c, :, at:at + width] = value[8 * c:8 * c + RAW].astype(BF16)
-    beside = jnp.where(above, 1, 0) + jnp.where(below, 1, 0) + jnp.where(core == 1, jnp.where(above, 1, 0), jnp.where(below, 1, 0))
-    pl.semaphore_wait(barrier, lines - 1 + columns - 1 + 1 + beside)
+
+    big.wait()
+    for p in range(len(fine) - 1):
+        refine(p)
+    pl.semaphore_wait(barrier, lines - 1 + columns - 1 + 1 + 2 * (jnp.where(above, 1, 0) + jnp.where(below, 1, 0)))
 
     def halo_up(p):
         return pltpu.make_async_remote_copy(
@@ -221,76 +218,80 @@
 
     def junction(dy, dx):
         i = dy * columns + dx
-        sems = junction_send.at[i], junction_recv.at[i]
-        if dy == 0:
-            return pltpu.make_async_remote_copy(
-                jsend.at[turn(column, dx, columns)], mid.at[:, column], *sems,
-                device_id=across(0, dx), device_id_type=MESH)
-        if dx == 0:
-            return pltpu.make_async_remote_copy(
-                jsend.at[column, turn(line, dy, lines)], jrecv.at[line, column], *sems,
-                device_id=across(dy, 0), device_id_type=MESH)
-        came = turn(column, -dx, columns)
-        return pltpu.make_async_remote_copy(
-            mid.at[turn(line, dy, lines), came], jrecv.at[line, came], *sems,
-            device_id=across(dy, 0), device_id_type=MESH)
+        return pltpu.make_async_remote_copy(
+            jsend.at[across(dy, dx)["seg"]], jrecv.at[seg], junction_send.at[i], junction_recv.at[i],
+            device_id=across(dy, dx), device_id_type=MESH)
 
     def junction_in(dy, dx):
         i = dy * columns + dx
-        sems = junction_send.at[i], junction_recv.at[i]
-        came = turn(column, -dx, columns)
-        if dy == 0:
-            return pltpu.make_async_remote_copy(
-                jsend.at[0], mid.at[:, came], *sems, device_id=across(0, dx), device_id_type=MESH)
-        return pltpu.make_async_remote_copy(
-            jsend.at[0, 0], jrecv.at[turn(line, -dy, lines), came], *sems,
-            device_id=across(dy, 0), device_id_type=MESH)
+        return pltpu.make_async_remote_copy(
+            jsend.at[seg], jrecv.at[across(-dy, -dx)["seg"]], junction_send.at[i], junction_recv.at[i],
+            device_id=across(dy, dx), device_id_type=MESH)
 
     steps = [(dy, dx) for dy in range(lines) for dx in range(columns) if dy + dx > 0]
 
-    def pass_junctions():
-        for dx in range(1, columns):
-            junction_in(0, dx).wait_recv()
-            for dy in range(1, lines):
-                junction(dy, dx).start()
-
-    def wall_swap(of):
-        slot = pl.ds(of * per_slab, per_slab)
-        return pltpu.make_async_remote_copy(
-            walls.at[slot], walls.at[slot], wall_send.at[0], wall_recv.at[0],
+    def wall(device):
+        slot = pl.ds(slab * per_slab, per_slab)
+        return pltpu.make_async_remote_copy(
+            walls.at[slot], walls.at[slot], wall_send.at[0], wall_recv.at[0], device_id=device, device_id_type=MESH)
+
+    def walls_all():
+        slots = pl.ds(0, (slabs - 1) * per_slab)
+        return pltpu.make_async_remote_copy(
+            walls.at[slots], walls.at[slots], wall_send.at[0], wall_recv.at[0],
             device_id={"slab": partner}, device_id_type=MESH)
 
-    def wall(t, way, of):
-        slot = pl.ds(of * (CORES * per_slab), CORES * per_slab)
-        send, recv = (up_send, up_recv) if way > 0 else (down_send, down_recv)
-        return pltpu.make_async_remote_copy(
-            walls.at[slot], walls.at[slot], send.at[t], recv.at[t],
-            device_id={"slab": slab + way * CORES}, device_id_type=MESH)
-
-    def wall_sends(t):
-        return [(above & (level >= t), wall(t, 1, level - t)), (below & (level + t < levels), wall(t, -1, level + t))]
-
-    def wall_arrivals(t):
-        return [(level > t, wall(t, 1, level - 1 - t)), (level + 1 + t < levels, wall(t, -1, level + 1 + t))]
-
-    def pass_walls(t):
-        if t == 0:
-            wall_swap(partner).wait_recv()
-        else:
-            for there, copy in wall_arrivals(t - 1):
-                pl.when(there)(copy.wait_recv)
-        if t < levels - 1:
-            for there, copy in wall_sends(t):
-                pl.when(there)(copy.start)
-
-    for p in range(len(fine)):
+    def wall_to(o):
+        @pl.when((level + o >= 0) & (level + o < levels))
+        def _():
+            wall({"slab": slab + o * CORES}).start()
+            wall({"slab": partner + o * CORES}).start()
+
+    def vouch(t):
+        @pl.when(below & (level + t < levels))
+        def _():
+            pl.semaphore_signal(above_in.at[t], inc=1, device_id={"slab": slab - CORES}, device_id_type=MESH)
+
+        @pl.when(above & (level - t >= 0))
+        def _():
+            pl.semaphore_signal(below_in.at[t], inc=1, device_id={"slab": slab + CORES}, device_id_type=MESH)
+
+    def vouched(t):
+        @pl.when(level + 1 + t < levels)
+        def _():
+            pl.semaphore_wait(above_in.at[t], 1)
+
+        @pl.when(level - 1 - t >= 0)
+        def _():
+            pl.semaphore_wait(below_in.at[t], 1)
+
+    def send_halo(p):
         pl.when(slab < slabs - 1)(halo_up(p).start)
         pl.when(slab > 0)(halo_down(p).start)
+
     for dx in range(1, columns):
-        junction(0, dx).start()
-    for dy in range(1, lines):
-        junction(dy, 0).start()
-    wall_swap(slab).start()
+        pl.semaphore_signal(column_in.at[dx], inc=1, device_id=across(0, dx), device_id_type=MESH)
+    vouch(1)
+    for p in range(len(fine) - 1):
+        send_halo(p)
+    for dy, dx in steps:
+        if min(dy, dx) == 0:
+            junction(dy, dx).start()
+    wall({"slab": partner}).start()
+    wall_to(1)
+    wall_to(-1)
+    refine(len(fine) - 1)
+    send_halo(len(fine) - 1)
+    for dx in range(1, columns):
+        pl.semaphore_wait(column_in.at[dx], 1)
+        for dy in range(1, lines):
+            junction(dy, columns - dx).start()
+    for t in range(1, levels - 1):
+        vouched(t)
+        if t < levels - 2:
+            vouch(t + 1)
+        wall_to(t + 1)
+        wall_to(-1 - t)
 
     def repeat(raw):
         return jnp.dot(chosen, raw, preferred_element_type=F32)
@@ -307,7 +308,6 @@
         return sums[0:TERMS] + sums[TERMS:2 * TERMS] + sums[2 * TERMS:3 * TERMS]
 
     totals = {}
-    pass_walls(0)
 
     def run(units, between):
         before = []
@@ -338,8 +338,7 @@
             prepare(k * qp + start, repeat(fine[p][pair_source[0, k]]), quad_row[:, start:start + size])
 
     def prepare_junction(i, dy, dx):
-        source = (mid if dy == 0 else jrecv)[turn(line, -dy, lines), turn(column, -dx, columns)]
-        prepare(pairs * qp + i * pt, repeat(source), coarse_row[...])
+        prepare(pairs * qp + i * pt, repeat(jrecv[across(-dy, -dx)["seg"]]), coarse_row[...])
 
     def prepare_walls():
         near_by = jnp.concatenate([walls[wall_near[0, n, c]] for c in range(count) for n in range(near)], axis=1)
@@ -351,8 +350,7 @@
 
     def arrive_junctions(which):
         for i in which:
-            if steps[i][0] > 0:
-                junction_in(*steps[i]).wait_recv()
+            junction_in(*steps[i]).wait_recv()
         for i in which:
             prepare_junction(i, *steps[i])
 
@@ -387,19 +385,9 @@
     when(0, *[functools.partial(f, 0) for f in (arrive, prepare_pairs)])
     for p in range(1, len(parts)):
         when(firsts[p - 1], functools.partial(arrive, p))
-        if p == min(2, last):
-            when(firsts[p - 1], pass_junctions)
-        if 1 < p <= levels - 1:
-            when(firsts[p - 1], functools.partial(pass_walls, p - 1))
         when(firsts[p - 1], functools.partial(prepare_pairs, p))
-    done = max(last - 1, 0)
-    if last == 0:
-        when(0, pass_junctions)
     when(firsts[last], functools.partial(arrive_junctions, direct))
-    if done + 1 < levels:
-        when(firsts[last], functools.partial(pass_walls, done + 1))
-    when(ends[0], functools.partial(arrive_junctions, relayed))
-    when(ends[1], *[functools.partial(pass_walls, t) for t in range(done + 2, levels)], prepare_walls)
+    when(ends[0], functools.partial(arrive_junctions, relayed), walls_all().wait_recv, prepare_walls)
     run(units, between)
 
     places = [(("pair", k), pair_target[0, k]) for k in range(pairs)]
@@ -425,10 +413,7 @@
         pl.when(slab > 0)(halo_down(p).wait_send)
     for dy, dx in steps:
         junction(dy, dx).wait_send()
-    wall_swap(slab).wait_send()
-    for t in range(levels - 1):
-        for there, copy in wall_sends(t):
-            pl.when(there)(copy.wait_send)
+    walls_all().wait_send()
 
 
 def local(segs, slabs, positions, density, upsample, quad_weights, coarse_weights, pair_target, pair_source,
@@ -440,8 +425,7 @@
     per_slab, patch = wall_points.shape[1], wall_points.shape[3]
     cfg = (count, points, fine_points, pairs, near, patch, segs, slabs, per_slab)
     pt = up(points, LANES)
-    lines, columns = grid(segs)
-    levels = slabs // CORES
+    columns, levels = grid(segs)[1], slabs // CORES
     widths = [width for _, width in cuts(fine_points)]
     lanes = pairs * up(fine_points, LANES) + (segs - 1) * pt + count * near * up(patch, LANES)
     vmem = pl.BlockSpec(memory_space=pltpu.VMEM)
@@ -462,9 +446,8 @@
             pltpu.VMEM(coarse_weights.shape, F32),
             pltpu.VMEM((2,) + turned[1:], BF16),
             pltpu.VMEM((count, RAW, pt), BF16),
-            pltpu.VMEM((columns, lines, RAW, pt), BF16),
-            pltpu.VMEM((lines, columns, RAW, pt), BF16),
-            pltpu.VMEM((lines, columns, RAW, pt), BF16),
+            pltpu.VMEM((segs, RAW, pt), BF16),
+            pltpu.VMEM((segs, RAW, pt), BF16),
             pltpu.VMEM((2, per_slab, 3, patch), BF16),
             pltpu.VMEM((slabs * per_slab, RAW, patch), BF16),
             pltpu.VMEM(upsample.shape, BF16),
@@ -477,7 +460,7 @@
             pltpu.VMEM((TERMS, lanes), BF16),
             pltpu.VMEM((SPLITS * TERMS, lanes), BF16),
             dma((12,)), dma((2, len(widths))), dma((2, len(widths))), dma((segs,)), dma((segs,)), dma((1,)), dma((1,)),
-            dma((levels,)), dma((levels,)), dma((levels,)), dma((levels,)),
+            *[pltpu.SemaphoreType.REGULAR((n,)) for n in (columns, levels, levels)],
             *[pltpu.VMEM((count + 2 * HALO, RAW, width), BF16) for width in widths],
         ],
         compiler_params=pltpu.CompilerParams(collective_id=0, has_side_effects=True),

time: 17.4 us -> 14.7 us (0.84)
  Pallas kernels: 16.7 us -> 13.9 us
    pallas_call x1, Pallas kernels: 16.7 us -> 13.9 us  [local(): pl.pallas_call(functools.partial(kernel, cfg), out_shape=pltpu.VMEM(turne...]
where the time goes in v6:
time: 14.7 us; the launch traced here: 14.6 us
  Pallas kernels  13.9 us (95%)
  local copies, waits for them, and re-layouts  0.62 us (4%)
    pallas_call x1, Pallas kernels, local(): pl.pallas_call(functools.partial(kernel, cfg), out_shape=pltpu.VMEM(turne...  13.9 us
    unnamed x1, local copies, waits for them, and re-layouts  0.62 us

profile of v6, /device:TPU:0, one launch (start us, length us, event | category | flops | bytes accessed | tf_op | source)
XLA Modules:
  0.0 14.6 jit_solution(7226767559912917325)
XLA Ops:
  0.0 13.9 %shard_map.118 = f32[1,3,4,642]{3,2,1,0:T(4,128)S(1)} custom-call(s32[1,2]{1,0:T(1,128)} %pair_target_far.1, s32[1,2]{1,0:T(1,128)} %pair_source_far.1, s32[1,1,4]{2,1,0:T(1,128)} %junction_cell_far.1, s32[1,1,4]{2,1,0:T(1,128)} %junction_target_far.1, s32[1,2,4]{2,1,0:T(2,128)} %bitcast.7, bf16[1,3,4,642]{3,2,1,0:T(4,128)(2,1)} %bitcast.5, ...), custom_call_target="tpu_custom_call" | custom-call | tf_op jit(solution)/shard_map/pallas_call | solution.py:434
  13.9 0.6 %copy.14 = f32[1,4,3,642]{3,1,2,0:T(4,128)} copy(f32[1,4,3,642]{3,1,2,0:T(4,128)S(1)} %bitcast.4) | data formatting | bytes 61632

commit v7 on v6

--- a/solution.py
+++ b/solution.py
@@ -92,7 +92,7 @@
     out,
     pair_target, pair_source, junction_cell, junction_target, wall_near, quad, coarse,
     own, mine, jsend, jrecv, wall_own, walls, ups, rows, quad_row, coarse_row, xt, xs, held, nears, weights,
-    local_sem, halo_send, halo_recv, junction_send, junction_recv, wall_send, wall_recv, column_in, above_in, below_in, *fine,
+    local_sem, big_sem, halo_send, halo_recv, junction_send, junction_recv, wall_send, wall_recv, column_in, above_in, below_in, *fine,
 ):
     count, points, fine_points, pairs, near, patch, segs, slabs, per_slab = cfg
     pt, qp = xs.shape[2], quad_row.shape[1]
@@ -138,15 +138,17 @@
         pltpu.make_async_copy(wall_points.at[0], wall_own.at[0], local_sem.at[2]),
         pltpu.make_async_copy(wall_traction.at[0], wall_own.at[1], local_sem.at[3]),
     ]
-    big = pltpu.make_async_copy(upsample, ups, local_sem.at[4])
+    big = [
+        pltpu.make_async_copy(
+            upsample.at[:, start:min(start + size, fine_points)], ups.at[:, start:min(start + size, fine_points)], big_sem.at[i])
+        for i, (start, size) in enumerate(cuts(fine_points))]
     tables = [
         pltpu.make_async_copy(source, target, local_sem.at[5 + i]) for i, (source, target) in enumerate([
             (pair_target_far, pair_target), (pair_source_far, pair_source), (junction_cell_far, junction_cell),
             (junction_target_far, junction_target), (wall_near_far, wall_near), (quad_far, quad), (coarse_far, coarse)])
     ]
-    for copy in copies + tables:
+    for copy in copies + tables + big:
         copy.start()
-    big.start()
     for copy in copies + tables:
         copy.wait()
 
@@ -174,6 +176,120 @@
     for p in range(per_slab):
         walls[slab * per_slab + p] = jnp.concatenate(
             [wall_own[0, p].astype(F32), wall_own[1, p].astype(F32)], axis=0).astype(BF16)
+    def refine(p):
+        (start, size), part = parts[p], fine[p]
+        big[p].wait()
+        for at in range(0, size, WIDE):
+            stop = min(start + at + WIDE, fine_points)
+            value = jnp.dot(lhs, ups[:, start + at:stop], preferred_element_type=F32)
+            width = min(WIDE, size - at)
+            if stop - start - at < width:
+                value = jnp.concatenate([value, jnp.zeros((8 * count, width - value.shape[1]), F32)], axis=1)
+            for c in range(count):
+                part[HALO + c, :, at:at + width] = value[8 * c:8 * c + RAW].astype(BF16)
+
+    early = min(0, len(fine))
+    for p in range(early):
+        refine(p)
+    pl.semaphore_wait(barrier, lines - 1 + columns - 1 + 1 + 2 * (jnp.where(above, 1, 0) + jnp.where(below, 1, 0)))
+
+    def halo_up(p):
+        return pltpu.make_async_remote_copy(
+            fine[p].at[pl.ds(count, HALO)], fine[p].at[pl.ds(0, HALO)], halo_send.at[0, p], halo_recv.at[0, p],
+            device_id={"slab": lax.rem(slab + 1, slabs)}, device_id_type=MESH)
+
+    def halo_down(p):
+        return pltpu.make_async_remote_copy(
+            fine[p].at[pl.ds(HALO, HALO)], fine[p].at[pl.ds(HALO + count, HALO)], halo_send.at[1, p], halo_recv.at[1, p],
+            device_id={"slab": lax.rem(slab + slabs - 1, slabs)}, device_id_type=MESH)
+
+    def junction(dy, dx):
+        i = dy * columns + dx
+        return pltpu.make_async_remote_copy(
+            jsend.at[across(dy, dx)["seg"]], jrecv.at[seg], junction_send.at[i], junction_recv.at[i],
+            device_id=across(dy, dx), device_id_type=MESH)
+
+    def junction_in(dy, dx):
+        i = dy * columns + dx
+        return pltpu.make_async_remote_copy(
+            jsend.at[seg], jrecv.at[across(-dy, -dx)["seg"]], junction_send.at[i], junction_recv.at[i],
+            device_id=across(dy, dx), device_id_type=MESH)
+
+    steps = [(dy, dx) for dy in range(lines) for dx in range(columns) if dy + dx > 0]
+
+    def wall(device):
+        slot = pl.ds(slab * per_slab, per_slab)
+        return pltpu.make_async_remote_copy(
+            walls.at[slot], walls.at[slot], wall_send.at[0], wall_recv.at[0], device_id=device, device_id_type=MESH)
+
+    def walls_all():
+        slots = pl.ds(0, (slabs - 1) * per_slab)
+        return pltpu.make_async_remote_copy(
+            walls.at[slots], walls.at[slots], wall_send.at[0], wall_recv.at[0],
+            device_id={"slab": partner}, device_id_type=MESH)
+
+    def wall_to(o):
+        @pl.when((level + o >= 0) & (level + o < levels))
+        def _():
+            wall({"slab": slab + o * CORES}).start()
+            wall({"slab": partner + o * CORES}).start()
+
+    def vouch(t):
+        @pl.when(below & (level + t < levels))
+        def _():
+            pl.semaphore_signal(above_in.at[t], inc=1, device_id={"slab": slab - CORES}, device_id_type=MESH)
+
+        @pl.when(above & (level - t >= 0))
+        def _():
+            pl.semaphore_signal(below_in.at[t], inc=1, device_id={"slab": slab + CORES}, device_id_type=MESH)
+
+    def vouched(t):
+        @pl.when(level + 1 + t < levels)
+        def _():
+            pl.semaphore_wait(above_in.at[t], 1)
+
+        @pl.when(level - 1 - t >= 0)
+        def _():
+            pl.semaphore_wait(below_in.at[t], 1)
+
+    def send_halo(p):
+        pl.when(slab < slabs - 1)(halo_up(p).start)
+        pl.when(slab > 0)(halo_down(p).start)
+
+    for dx in range(1, columns):
+        pl.semaphore_signal(column_in.at[dx], inc=1, device_id=across(0, dx), device_id_type=MESH)
+    vouch(1)
+    for p in range(early):
+        send_halo(p)
+    for dy, dx in steps:
+        if min(dy, dx) == 0:
+            junction(dy, dx).start()
+    wall({"slab": partner}).start()
+    wall_to(1)
+    wall_to(-1)
+    def cross():
+        for dx in range(1, columns):
+            pl.semaphore_wait(column_in.at[dx], 1)
+            for dy in range(1, lines):
+                junction(dy, columns - dx).start()
+
+    def reach(stages):
+        for t in stages:
+            vouched(t)
+            if t < levels - 2:
+                vouch(t + 1)
+            wall_to(t + 1)
+            wall_to(-1 - t)
+
+    def halo(chosen_parts):
+        for p in chosen_parts:
+            refine(p)
+            send_halo(p)
+
+    stages, every = range(1, levels - 1), range(len(fine))
+    halo(every[0:1])
+    halo(every[1:2])
+    halo(every[2:])
     chosen = spread()
     quad_row[...] = jnp.zeros_like(quad_row)
     coarse_row[...] = jnp.zeros_like(coarse_row)
@@ -190,109 +306,8 @@
             rows[3 + i:4 + i, 0:points] = norms[i][c:c + 1]
         xt[c] = rows[...].T[0:rows_t].astype(BF16)
 
-    def refine(p):
-        (start, size), part = parts[p], fine[p]
-        for at in range(0, size, WIDE):
-            stop = min(start + at + WIDE, fine_points)
-            value = jnp.dot(lhs, ups[:, start + at:stop], preferred_element_type=F32)
-            width = min(WIDE, size - at)
-            if stop - start - at < width:
-                value = jnp.concatenate([value, jnp.zeros((8 * count, width - value.shape[1]), F32)], axis=1)
-            for c in range(count):
-                part[HALO + c, :, at:at + width] = value[8 * c:8 * c + RAW].astype(BF16)
-
-    big.wait()
-    for p in range(len(fine) - 1):
-        refine(p)
-    pl.semaphore_wait(barrier, lines - 1 + columns - 1 + 1 + 2 * (jnp.where(above, 1, 0) + jnp.where(below, 1, 0)))
-
-    def halo_up(p):
-        return pltpu.make_async_remote_copy(
-            fine[p].at[pl.ds(count, HALO)], fine[p].at[pl.ds(0, HALO)], halo_send.at[0, p], halo_recv.at[0, p],
-            device_id={"slab": lax.rem(slab + 1, slabs)}, device_id_type=MESH)
-
-    def halo_down(p):
-        return pltpu.make_async_remote_copy(
-            fine[p].at[pl.ds(HALO, HALO)], fine[p].at[pl.ds(HALO + count, HALO)], halo_send.at[1, p], halo_recv.at[1, p],
-            device_id={"slab": lax.rem(slab + slabs - 1, slabs)}, device_id_type=MESH)
-
-    def junction(dy, dx):
-        i = dy * columns + dx
-        return pltpu.make_async_remote_copy(
-            jsend.at[across(dy, dx)["seg"]], jrecv.at[seg], junction_send.at[i], junction_recv.at[i],
-            device_id=across(dy, dx), device_id_type=MESH)
-
-    def junction_in(dy, dx):
-        i = dy * columns + dx
-        return pltpu.make_async_remote_copy(
-            jsend.at[seg], jrecv.at[across(-dy, -dx)["seg"]], junction_send.at[i], junction_recv.at[i],
-            device_id=across(dy, dx), device_id_type=MESH)
-
-    steps = [(dy, dx) for dy in range(lines) for dx in range(columns) if dy + dx > 0]
-
-    def wall(device):
-        slot = pl.ds(slab * per_slab, per_slab)
-        return pltpu.make_async_remote_copy(
-            walls.at[slot], walls.at[slot], wall_send.at[0], wall_recv.at[0], device_id=device, device_id_type=MESH)
-
-    def walls_all():
-        slots = pl.ds(0, (slabs - 1) * per_slab)
-        return pltpu.make_async_remote_copy(
-            walls.at[slots], walls.at[slots], wall_send.at[0], wall_recv.at[0],
-            device_id={"slab": partner}, device_id_type=MESH)
-
-    def wall_to(o):
-        @pl.when((level + o >= 0) & (level + o < levels))
-        def _():
-            wall({"slab": slab + o * CORES}).start()
-            wall({"slab": partner + o * CORES}).start()
-
-    def vouch(t):
-        @pl.when(below & (level + t < levels))
-        def _():
-            pl.semaphore_signal(above_in.at[t], inc=1, device_id={"slab": slab - CORES}, device_id_type=MESH)
-
-        @pl.when(above & (level - t >= 0))
-        def _():
-            pl.semaphore_signal(below_in.at[t], inc=1, device_id={"slab": slab + CORES}, device_id_type=MESH)
-
-    def vouched(t):
-        @pl.when(level + 1 + t < levels)
-        def _():
-            pl.semaphore_wait(above_in.at[t], 1)
-
-        @pl.when(level - 1 - t >= 0)
-        def _():
-            pl.semaphore_wait(below_in.at[t], 1)
-
-    def send_halo(p):
-        pl.when(slab < slabs - 1)(halo_up(p).start)
-        pl.when(slab > 0)(halo_down(p).start)
-
-    for dx in range(1, columns):
-        pl.semaphore_signal(column_in.at[dx], inc=1, device_id=across(0, dx), device_id_type=MESH)
-    vouch(1)
-    for p in range(len(fine) - 1):
-        send_halo(p)
-    for dy, dx in steps:
-        if min(dy, dx) == 0:
-            junction(dy, dx).start()
-    wall({"slab": partner}).start()
-    wall_to(1)
-    wall_to(-1)
-    refine(len(fine) - 1)
-    send_halo(len(fine) - 1)
-    for dx in range(1, columns):
-        pl.semaphore_wait(column_in.at[dx], 1)
-        for dy in range(1, lines):
-            junction(dy, columns - dx).start()
-    for t in range(1, levels - 1):
-        vouched(t)
-        if t < levels - 2:
-            vouch(t + 1)
-        wall_to(t + 1)
-        wall_to(-1 - t)
-
+    reach(stages[0:1])
+    cross()
     def repeat(raw):
         return jnp.dot(chosen, raw, preferred_element_type=F32)
 
@@ -383,6 +398,7 @@
 
     last = len(parts) - 1
     when(0, *[functools.partial(f, 0) for f in (arrive, prepare_pairs)])
+    when(0, functools.partial(reach, stages[1:]))
     for p in range(1, len(parts)):
         when(firsts[p - 1], functools.partial(arrive, p))
         when(firsts[p - 1], functools.partial(prepare_pairs, p))
@@ -459,7 +475,7 @@
             pltpu.VMEM((2, 2, up(points, 16), WIDE), BF16),
             pltpu.VMEM((TERMS, lanes), BF16),
             pltpu.VMEM((SPLITS * TERMS, lanes), BF16),
-            dma((12,)), dma((2, len(widths))), dma((2, len(widths))), dma((segs,)), dma((segs,)), dma((1,)), dma((1,)),
+            dma((12,)), dma((len(widths),)), dma((2, len(widths))), dma((2, len(widths))), dma((segs,)), dma((segs,)), dma((1,)), dma((1,)),
             *[pltpu.SemaphoreType.REGULAR((n,)) for n in (columns, levels, levels)],
             *[pltpu.VMEM((count + 2 * HALO, RAW, width), BF16) for width in widths],
         ],

time: 14.7 us -> 13.9 us (0.946)
  the two profiles are of different devices: /device:TPU:0 before, /device:TPU:1 now
where the time goes in v7:
time: 13.9 us; the launch traced here: 13.8 us
  Pallas kernels  13.2 us (95%)
  local copies, waits for them, and re-layouts  0.62 us (4%)
    pallas_call x1, Pallas kernels, local(): pl.pallas_call(functools.partial(kernel, cfg), out_shape=pltpu.VMEM(turne...  13.2 us
    unnamed x1, local copies, waits for them, and re-layouts  0.62 us

profile of v7, /device:TPU:1, one launch (start us, length us, event | category | flops | bytes accessed | tf_op | source)
XLA Modules:
  0.0 13.8 jit_solution(17482330668805697349)
XLA Ops:
  0.0 13.2 %shard_map.118 = f32[1,3,4,642]{3,2,1,0:T(4,128)S(1)} custom-call(s32[1,2]{1,0:T(1,128)} %pair_target_far.1, s32[1,2]{1,0:T(1,128)} %pair_source_far.1, s32[1,1,4]{2,1,0:T(1,128)} %junction_cell_far.1, s32[1,1,4]{2,1,0:T(1,128)} %junction_target_far.1, s32[1,2,4]{2,1,0:T(2,128)} %bitcast.7, bf16[1,3,4,642]{3,2,1,0:T(4,128)(2,1)} %bitcast.5, ...), custom_call_target="tpu_custom_call" | custom-call | tf_op jit(solution)/shard_map/pallas_call | solution.py:450
  13.2 0.6 %copy.14 = f32[1,4,3,642]{3,1,2,0:T(4,128)} copy(f32[1,4,3,642]{3,1,2,0:T(4,128)S(1)} %bitcast.4) | data formatting | bytes 61632

commit v8 on v7

--- a/solution.py
+++ b/solution.py
@@ -403,7 +403,8 @@
         when(firsts[p - 1], functools.partial(arrive, p))
         when(firsts[p - 1], functools.partial(prepare_pairs, p))
     when(firsts[last], functools.partial(arrive_junctions, direct))
-    when(ends[0], functools.partial(arrive_junctions, relayed), walls_all().wait_recv, prepare_walls)
+    when(ends[0], functools.partial(arrive_junctions, relayed))
+    when(ends[1], walls_all().wait_recv, prepare_walls)
     run(units, between)
 
     places = [(("pair", k), pair_target[0, k]) for k in range(pairs)]

time: 13.9 us -> 13.7 us (0.986)
  Pallas kernels: 13.2 us -> 12.9 us
    pallas_call x1, Pallas kernels: 13.2 us -> 12.9 us  [local(): pl.pallas_call(functools.partial(kernel, cfg), out_shape=pltpu.VMEM(turne...]
where the time goes in v8:
time: 13.7 us; the launch traced here: 13.6 us
  Pallas kernels  12.9 us (94%)
  local copies, waits for them, and re-layouts  0.62 us (5%)
    pallas_call x1, Pallas kernels, local(): pl.pallas_call(functools.partial(kernel, cfg), out_shape=pltpu.VMEM(turne...  12.9 us
    unnamed x1, local copies, waits for them, and re-layouts  0.62 us

profile of v8, /device:TPU:1, one launch (start us, length us, event | category | flops | bytes accessed | tf_op | source)
XLA Modules:
  0.0 13.6 jit_solution(10397207792277615375)
XLA Ops:
  0.0 12.9 %shard_map.118 = f32[1,3,4,642]{3,2,1,0:T(4,128)S(1)} custom-call(s32[1,2]{1,0:T(1,128)} %pair_target_far.1, s32[1,2]{1,0:T(1,128)} %pair_source_far.1, s32[1,1,4]{2,1,0:T(1,128)} %junction_cell_far.1, s32[1,1,4]{2,1,0:T(1,128)} %junction_target_far.1, s32[1,2,4]{2,1,0:T(2,128)} %bitcast.7, bf16[1,3,4,642]{3,2,1,0:T(4,128)(2,1)} %bitcast.5, ...), custom_call_target="tpu_custom_call" | custom-call | tf_op jit(solution)/shard_map/pallas_call | solution.py:451
  13.0 0.6 %copy.14 = f32[1,4,3,642]{3,1,2,0:T(4,128)} copy(f32[1,4,3,642]{3,1,2,0:T(4,128)S(1)} %bitcast.4) | data formatting | bytes 61632
